TPU v7x, 32 devices: a whole 2x2x4 slice. The times are simulated.
32 devices in a mesh: chan: 16 (over z, x, core), win: 2 (over y).
Axes of the slice: x: 2, y: 2, z: 4, core: 2. Of those that a mesh axis runs over, the one named last changes fastest.
Arguments:
- spectra: bfloat16 [8, 1024, 2, 2048], P('win', 'chan'), may hold values from -4.5 to 4.5
- owners: int32 [4], replicated, may hold values from 0 to 15
- blocks: int32 [4], replicated, may hold values from 0 to 3
- max_lag: int32 [4, 16, 1024], P(None, 'win', 'chan'), may hold values from 1 to 64
Outputs:
- correlations: float32 [4, 16, 1024, 128], P(None, 'win', 'chan')
All inputs are finite; a program needn't handle non-finite values.
Results may differ from a plain program's by a relative error of at most 0.0034.
Values may be sent and summed in bfloat16 or wider, within the bound.
A program may use at most 128 MiB of HBM per device.

v0:
```python
import jax
import jax.numpy as jnp
from jax import lax
from jax.sharding import PartitionSpec as P

SRC = 16
STEPS = 4
LAGS = 128


def from_root(value, axis, source):
    kept = jnp.where(lax.axis_index(axis) == source, value, 0).astype(value.dtype)
    return lax.psum(kept, axis)


def lag_table(bin_count, lag_count, window_count):
    bins = jnp.arange(bin_count, dtype=jnp.int32)[:, None]
    offsets = jnp.arange(lag_count, dtype=jnp.int32)[None, :] - lag_count // 2
    phase = (bins * offsets % (2 * bin_count)).astype(jnp.float32) * (jnp.pi / bin_count)
    weight = jnp.where(bins == 0, 1.0, 2.0).astype(jnp.float32) / jnp.sqrt(
        jnp.float32(2.0 * bin_count * window_count)
    )
    return jnp.concatenate([weight * jnp.cos(phase), -weight * jnp.sin(phase)], 0).astype(
        jnp.bfloat16
    )


def cross_spectra(source_block, receivers):
    window_count = source_block.shape[0]
    real_part = None
    imag_part = None
    for window in range(window_count):
        a_real = source_block[window, :, 0].astype(jnp.float32)[:, None, :]
        a_imag = source_block[window, :, 1].astype(jnp.float32)[:, None, :]
        b_real = receivers[window, :, 0][None, :, :]
        b_imag = receivers[window, :, 1][None, :, :]
        real_term = a_real * b_real + a_imag * b_imag
        imag_term = a_imag * b_real - a_real * b_imag
        real_part = real_term if real_part is None else real_part + real_term
        imag_part = imag_term if imag_part is None else imag_part + imag_term
    return jnp.stack([real_part, imag_part], 2).astype(jnp.bfloat16)


def body(spectra, owners, blocks, max_lag):
    window_count, channel_count, _, bin_count = spectra.shape
    group_count = lax.axis_size("win")
    lag_matrix = lag_table(bin_count, LAGS, window_count * group_count)

    def correlate(source_block):
        source_count = source_block.shape[1]
        cross_part = cross_spectra(source_block, spectra)
        flat = cross_part.reshape(source_count * channel_count, 2 * bin_count)
        product = jnp.dot(flat, lag_matrix, preferred_element_type=jnp.float32)
        return product.reshape(source_count, channel_count, LAGS)

    def pick(step_index):
        return lax.dynamic_slice_in_dim(spectra, blocks[step_index] * SRC, SRC, 1)

    def fetch(step_index):
        return from_root(pick(step_index), "chan", owners[step_index])

    incoming = [fetch(step_index) for step_index in range(STEPS)]

    def stack_step(source_all):
        return lax.psum_scatter(correlate(source_all), "win", scatter_dimension=0, tiled=True)

    stacked = jnp.stack([stack_step(incoming[step_index]) for step_index in range(STEPS)])
    offsets = jnp.abs(jnp.arange(LAGS, dtype=jnp.int32) - LAGS // 2)
    inside = offsets[None, None, None, :] <= max_lag[:, :, :, None]
    return jnp.where(inside, stacked, jnp.float32(0.0))


def solution(mesh):
    return jax.shard_map(
        body,
        mesh=mesh,
        in_specs=(P("win", "chan", None, None), P(), P(), P(None, "win", "chan")),
        out_specs=P(None, "win", "chan", None),
        check_vma=False,
    )
```

profile of v0, /device:TPU:0, one launch (start us, length us, event | category | flops | bytes accessed | tf_op | source)
XLA Modules:
  0.0 603.0 jit_solution(10538095125140154076)
XLA Ops:
  6.5 1.5 fusion.54
  10.7 1.5 fusion.53
  14.7 3.7 constant_dynamic-slice_fusion.3
  18.3 1.6 copy_select_fusion.2
  20.0 1.6 copy_select_fusion
  21.8 3.3 fusion.52
  25.2 0.4 fusion.6
  25.9 5.5 multiply_convert_fusion.1
  31.8 1.3 fusion.12
  33.1 89.6 %all-reduce.3.cloned.1.call-done = (bf16[4,16,2,2048]{3,1,2,0:T(8,128)(2,1)}, bf16[4,16,2,2048]{3,1,2,0:T(8,128)(2,1)}, bf16[4,16,2,2048]{3,1,2,0:T(8,128)(2,1)}, bf16[4,16,2,2048]{3,1,2,0:T(8,128)(2,1)}) async-done(((bf16[4,16,2,2048]{3,1,2,0:T(8,128)(2,1)}, bf16[4,16,2,2048]{3,1,2,0:T(8,128)(2,1)}, bf16[4,16,2,2048]{3,1,2,0:T(8,128)(2,1)}, bf16[4,16,2,2048]{3,1,2,0:T(8,128)(2,1)}), ...) | async-done | bytes 2097168 | tf_op jit(solution)/shard_map/psum | solution.py:13
  122.8 1.2 fusion.45
  123.9 71.6 %add_convert_fusion.7 = (bf16[16,64,1,2048]{3,2,1,0:T(2,128)(2,1)S(1)}, bf16[16,64,1,2048]{3,2,1,0:T(2,128)(2,1)}) fusion(f32[64,2048]{1,0:T(8,128)S(1)} %get-tuple-element.75, f32[16,2048]{1,0:T(8,128)S(1)} %get-tuple-element.30, f32[64,2048]{1,0:T(8,128)S(1)} %get-tuple-element.76, f32[16,2048]{1,0:T(8,128)S(1)} %get-tuple-element.31, ...), kind=kLoop, calls=%fused_computation.11 | loop fusion | flops 67108864 | bytes 13631488 | tf_op jit(solution)/shard_map/convert.48
  195.5 19.6 %pad_maximum_fusion = bf16[16,64,2,2048]{3,2,1,0:T(2,128)(2,1)} fusion(bf16[16,64,1,2048]{3,2,1,0:T(2,128)(2,1)} %get-tuple-element.10, bf16[16,64,1,2048]{3,2,1,0:T(2,128)(2,1)S(1)} %get-tuple-element.9), kind=kLoop, calls=%fused_computation | loop fusion | flops 16777216 | bytes 16777216 | tf_op jit(solution)/shard_map/stack | solution.py:41
  215.2 14.5 %convert_element_type.531 = bf16[16,64,4096]{2,1,0:T(8,128)(2,1)} reshape(bf16[16,64,2,2048]{3,2,1,0:T(2,128)(2,1)} %pad_maximum_fusion) | data formatting | bytes 16777216 | tf_op jit(solution)/shard_map/convert_element_type | solution.py:41
  229.7 6.7 %fusion.51 = f32[16,64,128]{2,1,0:T(8,128)} fusion(bf16[16,64,4096]{2,1,0:T(8,128)(2,1)} %convert_element_type.531, bf16[2048,128]{1,0:T(8,128)(2,1)} %get-tuple-element.62, bf16[2048,128]{1,0:T(8,128)(2,1)} %get-tuple-element.61), kind=kOutput, calls=%fused_computation.121 | convolution fusion | flops 1075838976 | bytes 9961472 | tf_op jit(solution)/shard_map/dot_general | solution.py:53
  236.4 1.2 fusion.37
  237.6 1.2 fusion.29
  238.8 71.8 %add_convert_fusion.5 = (bf16[16,64,1,2048]{3,2,1,0:T(2,128)(2,1)S(1)}, bf16[16,64,1,2048]{3,2,1,0:T(2,128)(2,1)}) fusion(f32[16,2048]{1,0:T(8,128)S(1)} %get-tuple-element.38, f32[16,2048]{1,0:T(8,128)S(1)} %get-tuple-element.39, f32[16,2048]{1,0:T(8,128)S(1)} %get-tuple-element.40, f32[16,2048]{1,0:T(8,128)S(1)} %get-tuple-element.41, ...), kind=kLoop, calls=%fused_computation.9 | loop fusion | flops 67108864 | bytes 13631488 | tf_op jit(solution)/shard_map/convert.44
  310.6 19.7 %pad_maximum_fusion.1 = bf16[16,64,2,2048]{3,2,1,0:T(2,128)(2,1)} fusion(bf16[16,64,1,2048]{3,2,1,0:T(2,128)(2,1)} %get-tuple-element.12, bf16[16,64,1,2048]{3,2,1,0:T(2,128)(2,1)S(1)} %get-tuple-element.11), kind=kLoop, calls=%fused_computation.1 | loop fusion | flops 16777216 | bytes 16777216 | tf_op jit(solution)/shard_map/stack | solution.py:41
  330.3 70.3 %add_convert_fusion.3 = (bf16[16,64,1,2048]{3,2,1,0:T(2,128)(2,1)S(1)}, bf16[16,64,1,2048]{3,2,1,0:T(2,128)(2,1)}) fusion(f32[16,2048]{1,0:T(8,128)S(1)} %get-tuple-element.46, f32[16,2048]{1,0:T(8,128)S(1)} %get-tuple-element.47, f32[16,2048]{1,0:T(8,128)S(1)} %get-tuple-element.48, f32[16,2048]{1,0:T(8,128)S(1)} %get-tuple-element.49, ...), kind=kLoop, calls=%fused_computation.7 | loop fusion | flops 67108864 | bytes 13631488 | tf_op jit(solution)/shard_map/convert.42
  400.6 19.6 %pad_maximum_fusion.2 = bf16[16,64,2,2048]{3,2,1,0:T(2,128)(2,1)} fusion(bf16[16,64,1,2048]{3,2,1,0:T(2,128)(2,1)} %get-tuple-element.14, bf16[16,64,1,2048]{3,2,1,0:T(2,128)(2,1)S(1)} %get-tuple-element.13), kind=kLoop, calls=%fused_computation.2 | loop fusion | flops 16777216 | bytes 16777216 | tf_op jit(solution)/shard_map/stack | solution.py:41
  420.2 14.5 %convert_element_type.549 = bf16[16,64,4096]{2,1,0:T(8,128)(2,1)} reshape(bf16[16,64,2,2048]{3,2,1,0:T(2,128)(2,1)} %pad_maximum_fusion.1) | data formatting | bytes 16777216 | tf_op jit(solution)/shard_map/convert_element_type | solution.py:41
  434.7 14.7 %convert_element_type.566 = bf16[16,64,4096]{2,1,0:T(8,128)(2,1)} reshape(bf16[16,64,2,2048]{3,2,1,0:T(2,128)(2,1)} %pad_maximum_fusion.2) | data formatting | bytes 16777216 | tf_op jit(solution)/shard_map/convert_element_type | solution.py:41
  449.4 6.7 %fusion.50 = f32[16,64,128]{2,1,0:T(8,128)} fusion(bf16[16,64,4096]{2,1,0:T(8,128)(2,1)} %convert_element_type.549, bf16[2048,128]{1,0:T(8,128)(2,1)} %get-tuple-element.62, bf16[2048,128]{1,0:T(8,128)(2,1)} %get-tuple-element.61), kind=kOutput, calls=%fused_computation.120 | convolution fusion | flops 1075838976 | bytes 9961472 | tf_op jit(solution)/shard_map/dot_general | solution.py:53
  456.1 1.9 fusion.21
  458.0 6.7 %fusion.49 = f32[16,64,128]{2,1,0:T(8,128)} fusion(bf16[16,64,4096]{2,1,0:T(8,128)(2,1)} %convert_element_type.566, bf16[2048,128]{1,0:T(8,128)(2,1)} %get-tuple-element.62, bf16[2048,128]{1,0:T(8,128)(2,1)} %get-tuple-element.61), kind=kOutput, calls=%fused_computation.119 | convolution fusion | flops 1075838976 | bytes 9961472 | tf_op jit(solution)/shard_map/dot_general | solution.py:53
  464.8 73.8 %add_convert_fusion.1 = (bf16[16,64,1,2048]{3,2,1,0:T(2,128)(2,1)S(1)}, bf16[16,64,1,2048]{3,2,1,0:T(2,128)(2,1)}) fusion(f32[16,2048]{1,0:T(8,128)S(1)} %get-tuple-element.54, f32[16,2048]{1,0:T(8,128)S(1)} %get-tuple-element.55, f32[16,2048]{1,0:T(8,128)} %get-tuple-element.56, f32[16,2048]{1,0:T(8,128)} %get-tuple-element.57, ...), kind=kLoop, calls=%fused_computation.5 | loop fusion | flops 67108864 | bytes 13631488 | tf_op jit(solution)/shard_map/convert.40
  538.6 19.6 %pad_maximum_fusion.3 = bf16[16,64,2,2048]{3,2,1,0:T(2,128)(2,1)} fusion(bf16[16,64,1,2048]{3,2,1,0:T(2,128)(2,1)} %get-tuple-element.16, bf16[16,64,1,2048]{3,2,1,0:T(2,128)(2,1)S(1)} %get-tuple-element.15), kind=kLoop, calls=%fused_computation.3 | loop fusion | flops 16777216 | bytes 16777216 | tf_op jit(solution)/shard_map/stack | solution.py:41
  558.2 14.6 %convert_element_type.583 = bf16[16,64,4096]{2,1,0:T(8,128)(2,1)} reshape(bf16[16,64,2,2048]{3,2,1,0:T(2,128)(2,1)} %pad_maximum_fusion.3) | data formatting | bytes 16777216 | tf_op jit(solution)/shard_map/convert_element_type | solution.py:41
  572.8 6.5 %fusion.48 = f32[16,64,128]{2,1,0:T(8,128)} fusion(bf16[16,64,4096]{2,1,0:T(8,128)(2,1)} %convert_element_type.583, bf16[2048,128]{1,0:T(8,128)(2,1)S(1)} %copy-done.4, bf16[2048,128]{1,0:T(8,128)(2,1)S(1)} %copy-done.3), kind=kOutput, calls=%fused_computation.118 | convolution fusion | flops 1075838976 | bytes 9961472 | tf_op jit(solution)/shard_map/dot_general | solution.py:53
  579.4 14.3 %reduce-scatter.11.cloned.1.call-done = f32[8,64,128]{2,1,0:T(8,128)} async-done(((f32[16,64,128]{2,1,0:T(8,128)}), f32[8,64,128]{2,1,0:T(8,128)}) %reduce-scatter.11.cloned.1.call-update) | async-done | bytes 262160 | tf_op jit(solution)/shard_map/reduce_scatter | solution.py:65
  593.7 2.3 maximum_select_fusion
  (30 shorter events, 1.3 us)
Async XLA Ops:
  6.5 15.3 %copy-start = (bf16[4,64,2,2048]{3,2,1,0:T(2,128)(2,1)S(1)}, bf16[4,64,2,2048]{3,2,1,0:T(2,128)(2,1)}, u32[]{:S(2)}) copy-start(bf16[4,64,2,2048]{3,2,1,0:T(2,128)(2,1)} %param.4) | copy-start | bytes 6291460
  6.5 116.2 %all-reduce.3.cloned.1.call-start = ((), (), s32[]{:S(2)}) async-start(), calls=%async_computation.8 | async-start | bytes 4194304 | tf_op jit(solution)/shard_map/psum | solution.py:13
  21.6 557.8 %reduce-scatter.5.cloned.1.call-start = ((), (), s32[]{:S(2)}) async-start(), calls=%async_computation.4 | async-start | bytes 786432 | tf_op jit(solution)/shard_map/reduce_scatter | solution.py:65
  236.4 343.0 %reduce-scatter.7.cloned.1.call-start = ((), (), s32[]{:S(2)}) async-start(), calls=%async_computation.5 | async-start | bytes 786432 | tf_op jit(solution)/shard_map/reduce_scatter | solution.py:65
  310.6 19.7 %copy-start.1 = (f32[64,2048]{1,0:T(8,128)S(1)}, f32[64,2048]{1,0:T(8,128)}, u32[]{:S(2)}) copy-start(f32[64,2048]{1,0:T(8,128)} %get-tuple-element.81) | copy-start | bytes 1572868
  310.6 19.7 %copy-start.2 = (f32[64,2048]{1,0:T(8,128)S(1)}, f32[64,2048]{1,0:T(8,128)}, u32[]{:S(2)}) copy-start(f32[64,2048]{1,0:T(8,128)} %get-tuple-element.82) | copy-start | bytes 1572868
  456.1 123.3 %reduce-scatter.9.cloned.1.call-start = ((), (), s32[]{:S(2)}) async-start(), calls=%async_computation.6 | async-start | bytes 786432 | tf_op jit(solution)/shard_map/reduce_scatter | solution.py:65
  464.8 128.9 %reduce-scatter.11.cloned.1.call-start = ((), (), s32[]{:S(2)}) async-start(), calls=%async_computation.7 | async-start | bytes 786432 | tf_op jit(solution)/shard_map/reduce_scatter | solution.py:65
  558.2 14.6 %copy-start.3 = (bf16[2048,128]{1,0:T(8,128)(2,1)S(1)}, bf16[2048,128]{1,0:T(8,128)(2,1)}, u32[]{:S(2)}) copy-start(bf16[2048,128]{1,0:T(8,128)(2,1)} %get-tuple-element.61) | copy-start | bytes 1572868
  558.2 14.6 %copy-start.4 = (bf16[2048,128]{1,0:T(8,128)(2,1)S(1)}, bf16[2048,128]{1,0:T(8,128)(2,1)}, u32[]{:S(2)}) copy-start(bf16[2048,128]{1,0:T(8,128)(2,1)} %get-tuple-element.62) | copy-start | bytes 1572868
  572.8 20.9 %copy-start.5 = (s32[4,8,64]{2,1,0:T(8,128)S(1)}, s32[4,8,64]{2,1,0:T(8,128)}, u32[]{:S(2)}) copy-start(s32[4,8,64]{2,1,0:T(8,128)} %param.7) | copy-start | bytes 24580
Sparse Core Ops, SparseCore 0:
  21.7 101.0 all-reduce.2
  236.5 14.1 reduce-scatter.4
  456.2 14.1 reduce-scatter.6
  472.6 14.5 reduce-scatter.8
  579.5 14.1 reduce-scatter.10
where the time goes:
time: 608 us; the launch traced here: 603 us
  other arithmetic  385 us (63%)
  waiting for transfers between devices  104 us (17%)
  local copies, waits for them, and re-layouts  68.3 us (11%)
  matrix products  26.6 us (4%)
  between operations  18.9 us (3%)
    another operation x5, other arithmetic  293 us
    psum x1, waiting for transfers between devices, from_root(): return lax.psum(kept, axis)  89.6 us
    another operation x4, other arithmetic, cross_spectra(): return jnp.stack([real_part, imag_part], 2).astype(jnp.bfloat16)  78.5 us
    convert_element_type x4, local copies, waits for them, and re-layouts, cross_spectra(): return jnp.stack([real_part, imag_part], 2).astype(jnp.bfloat16)  58.3 us
    dot_general x4, matrix products, correlate(): product = jnp.dot(flat, lag_matrix, preferred_element_type=jnp.float32)  26.6 us
    reduce_scatter x4, waiting for transfers between devices, stack_step(): lax.psum_scatter(correlate(source_all), 'win', scatter_dimension=0, tiled...  14.3 us
  transfers between devices with their start and end apart: 5, of which 2 were waited for; matrix products, arithmetic and copies ran while one was open for 59% of the time, Pallas kernels for 0%

commit v1 on v0

v1 whole, which is shorter than its diff:
```python
import functools

import jax
import jax.numpy as jnp
from jax import lax
from jax.experimental import pallas as pl
from jax.experimental.pallas import tpu as pltpu
from jax.sharding import PartitionSpec as P

SRC = 16
STEPS = 4
LAGS = 128
LANES = 128


def from_root(value, axis, source):
    kept = jnp.where(lax.axis_index(axis) == source, value, 0).astype(value.dtype)
    return lax.psum(kept, axis)


def lag_table(bin_count, lag_count, window_count):
    bins = jnp.arange(bin_count, dtype=jnp.int32)[:, None]
    offsets = jnp.arange(lag_count, dtype=jnp.int32)[None, :] - lag_count // 2
    phase = (bins * offsets % (2 * bin_count)).astype(jnp.float32) * (jnp.pi / bin_count)
    weight = jnp.where(bins == 0, 1.0, 2.0).astype(jnp.float32) / jnp.sqrt(
        jnp.float32(2.0 * bin_count * window_count)
    )
    return jnp.concatenate([weight * jnp.cos(phase), -weight * jnp.sin(phase)], 1).astype(
        jnp.bfloat16
    )


def step_kernel(src_ref, recv_ref, lag_ref, out_ref, cross, *, terms, run, receivers):
    groups, sources, width = src_ref.shape
    lane = lax.broadcasted_iota(jnp.int32, (run, width), 1) % run
    row = lax.broadcasted_iota(jnp.int32, (run, width), 0)
    keep = (lane == row).astype(jnp.float32)
    zero = jnp.zeros((LANES, LANES), jnp.bfloat16)

    def group_step(g, carry):
        base = pl.multiple_of(g * 2 * run, 2 * run)
        first = jnp.concatenate([recv_ref[i, pl.ds(base, run), :] for i in range(terms)], 0)
        second = jnp.concatenate(
            [recv_ref[i, pl.ds(base + run, run), :] for i in range(terms)], 0
        )
        weight = jnp.concatenate(
            [jnp.concatenate([first, zero], 1), jnp.concatenate([zero, second], 1)], 0
        )
        values = src_ref[g].astype(jnp.float32)
        rows = jnp.concatenate(
            [
                (jnp.broadcast_to(values[s : s + 1], (run, width)) * keep).astype(jnp.bfloat16)
                for s in range(sources)
            ],
            0,
        )
        made = jnp.dot(rows, weight, preferred_element_type=jnp.float32).astype(jnp.bfloat16)
        for s in range(sources):
            part = made[s * run : (s + 1) * run]
            cross[pl.ds(base, run), s * LANES : (s + 1) * LANES] = part[:, :LANES]
            cross[pl.ds(base + run, run), s * LANES : (s + 1) * LANES] = part[:, LANES:]
        return carry

    lax.fori_loop(0, groups, group_step, 0, unroll=2)

    for pair in range(sources // 2):
        block = jnp.dot(
            lag_ref[...],
            cross[:, pair * 2 * LANES : (pair + 1) * 2 * LANES],
            preferred_element_type=jnp.float32,
        )
        turned = block.T
        lags = turned.shape[1] // 2
        for k in range(2):
            top = k * LANES
            out_ref[2 * pair + k] = (
                turned[top : top + receivers, :lags]
                + turned[top + receivers : top + 2 * receivers, lags:]
            )


def correlate(sources, received, lag_rows, receivers, run):
    groups, count, width = sources.shape
    terms, bins, _ = received.shape
    lags = lag_rows.shape[0] // 2
    return pl.pallas_call(
        functools.partial(step_kernel, terms=terms, run=run, receivers=receivers),
        out_shape=jax.ShapeDtypeStruct((count, receivers, lags), jnp.float32),
        in_specs=[pl.BlockSpec(memory_space=pltpu.VMEM)] * 3,
        out_specs=pl.BlockSpec(memory_space=pltpu.VMEM),
        scratch_shapes=[pltpu.VMEM((bins, count * LANES), jnp.bfloat16)],
        compiler_params=pltpu.CompilerParams(vmem_limit_bytes=40 << 20),
        cost_estimate=pl.CostEstimate(
            flops=8 * count * receivers * bins * lags,
            bytes_accessed=2 * (sources.size + received.size + lag_rows.size)
            + 4 * count * receivers * lags,
            transcendentals=0,
        ),
    )(sources, received, lag_rows)


def body(spectra, owners, blocks, max_lag):
    window_count, channel_count, _, bin_count = spectra.shape
    group_count = lax.axis_size("win")
    terms = 2 * window_count
    run = LANES // terms
    groups = bin_count // (2 * run)
    lag_rows = lag_table(bin_count, LAGS, window_count * group_count).T

    laid = spectra.reshape(window_count, channel_count, 2, groups, 2, run)
    laid = laid.transpose(3, 1, 4, 0, 2, 5).reshape(groups, channel_count, 2 * LANES)

    turned = spectra.transpose(0, 2, 3, 1)
    real, imag = turned[:, 0], turned[:, 1]
    received = jnp.stack(
        [jnp.concatenate([real, -imag], -1), jnp.concatenate([imag, real], -1)], 1
    ).reshape(terms, bin_count, 2 * channel_count)

    def pick(step_index):
        return lax.dynamic_slice_in_dim(laid, blocks[step_index] * SRC, SRC, 1)

    def fetch(step_index):
        return from_root(pick(step_index), "chan", owners[step_index])

    incoming = [fetch(step_index) for step_index in range(STEPS)]

    def stack_step(source_all):
        made = correlate(source_all, received, lag_rows, channel_count, run)
        return lax.psum_scatter(made, "win", scatter_dimension=0, tiled=True)

    stacked = jnp.stack([stack_step(incoming[step_index]) for step_index in range(STEPS)])
    offsets = jnp.abs(jnp.arange(LAGS, dtype=jnp.int32) - LAGS // 2)
    inside = offsets[None, None, None, :] <= max_lag[:, :, :, None]
    return jnp.where(inside, stacked, jnp.float32(0.0))


def solution(mesh):
    return jax.shard_map(
        body,
        mesh=mesh,
        in_specs=(P("win", "chan", None, None), P(), P(), P(None, "win", "chan")),
        out_specs=P(None, "win", "chan", None),
        check_vma=False,
    )
```

time: 608 us -> 249 us (0.41)
  other arithmetic: 385 us -> 13.2 us
  Pallas kernels: 0 us -> 45.4 us
  matrix products: 26.6 us -> 0 us
  local copies, waits for them, and re-layouts: 68.3 us -> 61.9 us
    another operation x9 -> x3, other arithmetic: 371 us -> 7.61 us
    convert_element_type x4 -> x0, local copies, waits for them, and re-layouts: 58.3 us -> none  [cross_spectra(): return jnp.stack([real_part, imag_part], 2).astype(jnp.bfloat16)]
    pallas_call x0 -> x4, Pallas kernels: none -> 45.4 us  [correlate(): pl.pallas_call(functools.partial(step_kernel, terms=terms, run=run, recei...]
    unnamed x12 -> x28, local copies, waits for them, and re-layouts: 0.02 us -> 33.5 us
    dot_general x4 -> x0, matrix products: 26.6 us -> none  [correlate(): product = jnp.dot(flat, lag_matrix, preferred_element_type=jnp.float32)]
    dynamic_slice x1, local copies, waits for them, and re-layouts: 3.67 us -> 14.6 us  [pick(): return lax.dynamic_slice_in_dim(laid, blocks[step_index] * SRC, SRC, 1)]
    reduce_scatter x4, waiting for transfers between devices: 14.3 us -> 23.5 us  [stack_step(): return lax.psum_scatter(made, 'win', scatter_dimension=0, tiled=True)]
    convert_element_type x8 -> x0, other arithmetic: 7.83 us -> none  [the longest x4 5.38 us: cross_spectra(): a_real = source_block[window, :, 0].astype(jnp.float32)[:, None, :]]
  transfers between devices with their start and end apart: 5 -> 5, of which waited for: 2 -> 3; matrix products, arithmetic and copies ran while one was open for 59% -> 6% of each run, Pallas kernels for 0% -> 14%
where the time goes in v1:
time: 249 us; the launch traced here: 248 us
  waiting for transfers between devices  109 us (44%)
  local copies, waits for them, and re-layouts  61.9 us (25%)
  Pallas kernels  45.4 us (18%)
  between operations  18.4 us (7%)
  other arithmetic  13.2 us (5%)
    psum x1, waiting for transfers between devices, from_root(): return lax.psum(kept, axis)  85.4 us
    pallas_call x4, Pallas kernels, correlate(): pl.pallas_call(functools.partial(step_kernel, terms=terms, run=run, recei...  45.4 us
    unnamed x28, local copies, waits for them, and re-layouts  33.5 us
    reduce_scatter x4, waiting for transfers between devices, stack_step(): return lax.psum_scatter(made, 'win', scatter_dimension=0, tiled=True)  23.5 us
    dynamic_slice x1, local copies, waits for them, and re-layouts, pick(): return lax.dynamic_slice_in_dim(laid, blocks[step_index] * SRC, SRC, 1)  14.6 us
    another operation x1, local copies, waits for them, and re-layouts, body(): jnp.stack([jnp.concatenate([real, -imag], -1), jnp.concatenate([imag, rea...  6.25 us
    transpose x1, local copies, waits for them, and re-layouts, body(): laid.transpose(3, 1, 4, 0, 2, 5).reshape(groups, channel_count, 2 * LANES)  5.42 us
  transfers between devices with their start and end apart: 5, of which 3 were waited for; matrix products, arithmetic and copies ran while one was open for 6% of the time, Pallas kernels for 14%

profile of v1, /device:TPU:0, one launch (start us, length us, event | category | flops | bytes accessed | tf_op | source)
XLA Modules:
  0.0 248.3 jit_solution(17295097821154486459)
XLA Ops:
  6.5 1.5 fusion.10
  10.5 6.9 %copy.8 = bf16[4,64,2,2048]{1,3,2,0:T(8,128)(2,1)} copy(bf16[4,64,2,2048]{3,2,1,0:T(2,128)(2,1)} %param.4) | data formatting | bytes 4194304 | tf_op args[0]
  17.4 5.4 %copy.9 = bf16[64,64,2,4,2,16]{1,5,4,3,2,0:T(8,128)(2,1)} copy(bf16[64,64,2,4,2,16]{1,5,2,0,4,3:T(8,128)(2,1)} %bitcast.37) | data formatting | bytes 4194304 | tf_op jit(solution)/shard_map/transpose | solution.py:111
  22.8 14.6 %constant_dynamic-slice_fusion.3 = (bf16[64,16,256]{1,2,0:T(8,128)(2,1)}, bf16[64,16,256]{1,2,0:T(8,128)(2,1)}, bf16[64,16,256]{1,2,0:T(8,128)(2,1)}, bf16[64,16,256]{1,2,0:T(8,128)(2,1)}) fusion(bf16[64,64,256]{1,2,0:T(8,128)(2,1)} %bitcast.36, s32[]{:T(128)S(6)} %select_n.66, s32[]{:T(128)S(6)} %select_n.74, s32[]{:T(128)S(6)} %select_n.71, s32[]{:T(128)S(6)} %select_n.77), kind=kLoop, calls=%fused_computation.29 | loop fusion | bytes 4194320 | tf_op jit(solution)/shard_map/dynamic_slice | solution.py:120
  37.4 3.5 %copy.16 = bf16[64,16,256]{2,1,0:T(8,128)(2,1)S(1)} copy(bf16[64,16,256]{1,2,0:T(8,128)(2,1)} %get-tuple-element.9) | data formatting | bytes 1048576
  40.9 3.5 %copy.17 = bf16[64,16,256]{2,1,0:T(8,128)(2,1)S(1)} copy(bf16[64,16,256]{1,2,0:T(8,128)(2,1)} %get-tuple-element.11) | data formatting | bytes 1048576
  44.4 0.6 fusion.9
  46.2 4.5 %copy.18 = bf16[64,16,256]{2,1,0:T(8,128)(2,1)} copy(bf16[64,16,256]{1,2,0:T(8,128)(2,1)} %get-tuple-element.10) | data formatting | bytes 1048576
  50.7 4.5 %copy.19 = bf16[64,16,256]{2,1,0:T(8,128)(2,1)} copy(bf16[64,16,256]{1,2,0:T(8,128)(2,1)} %get-tuple-element.12) | data formatting | bytes 1048576
  56.5 1.0 broadcast_select_fusion.2
  57.5 2.1 broadcast_select_fusion
  59.7 0.9 copy.21
  60.6 0.1 slice_bitcast_fusion
  60.7 0.1 fusion.8
  60.8 0.7 maximum_bitcast_fusion
  61.5 2.4 pad_maximum_fusion
  63.9 6.3 %copy.12 = bf16[4,2,2048,128]{3,2,1,0:T(8,128)(2,1)} copy(bf16[4,2,2048,128]{2,3,0,1:T(8,128)(2,1)} %pad_maximum_fusion) | data formatting | bytes 8388608 | tf_op jit(solution)/shard_map/stack | solution.py:115
  70.2 4.5 %multiply_convert_fusion.1 = (bf16[2048,128]{0,1:T(8,128)(2,1)S(1)}, bf16[2048,128]{0,1:T(8,128)(2,1)S(1)}) fusion(s32[128]{0:T(128)S(1)} %iota_add_fusion, f32[2048]{0:T(1024)S(1)} %get-tuple-element.31, f32[2048]{0:T(1024)S(1)} %get-tuple-element.32), kind=kLoop, calls=%fused_computation.15 | loop fusion | flops 4718592 | bytes 1065472 | tf_op jit(solution)/shard_map/convert
  74.8 85.4 %all-reduce.3.cloned.1.call-done = (bf16[64,16,256]{2,1,0:T(8,128)(2,1)}, bf16[64,16,256]{2,1,0:T(8,128)(2,1)}, bf16[64,16,256]{2,1,0:T(8,128)(2,1)}, bf16[64,16,256]{2,1,0:T(8,128)(2,1)}) async-done(((bf16[64,16,256]{2,1,0:T(8,128)(2,1)}, bf16[64,16,256]{2,1,0:T(8,128)(2,1)}, bf16[64,16,256]{2,1,0:T(8,128)(2,1)}, bf16[64,16,256]{2,1,0:T(8,128)(2,1)}), (bf16[64,16,256]{2,1,0:T(8,128)(2,1)}, ...) | async-done | bytes 2097168 | tf_op jit(solution)/shard_map/psum | solution.py:18
  160.2 2.2 copy-done
  162.4 1.0 copy-done.7
  163.5 11.4 %shard_map.46 = f32[16,64,128]{2,1,0:T(8,128)} custom-call(bf16[64,16,256]{2,1,0:T(8,128)(2,1)S(1)} %copy-done.7, bf16[8,2048,128]{2,1,0:T(8,128)(2,1)S(1)} %bitcast.32, bf16[256,2048]{1,0:T(8,128)(2,1)S(1)} %maximum_bitcast_fusion.2.lag_ref), custom_call_target="tpu_custom_call" | custom-call | flops 2147483648 | bytes 6291456 | tf_op jit(solution)/shard_map/pallas_call | solution.py:86
  174.8 0.2 reduce-scatter.7.cloned.1.call-start
  175.1 2.2 copy-done.1
  177.3 11.3 %shard_map.47 = f32[16,64,128]{2,1,0:T(8,128)} custom-call(bf16[64,16,256]{2,1,0:T(8,128)(2,1)S(1)} %copy-done.6, bf16[8,2048,128]{2,1,0:T(8,128)(2,1)S(1)} %bitcast.33, bf16[256,2048]{1,0:T(8,128)(2,1)S(1)} %maximum_bitcast_fusion.2.lag_ref), custom_call_target="tpu_custom_call" | custom-call | flops 2147483648 | bytes 6291456 | tf_op jit(solution)/shard_map/pallas_call | solution.py:86
  188.7 2.2 copy-done.2
  190.9 11.3 %shard_map.48 = f32[16,64,128]{2,1,0:T(8,128)} custom-call(bf16[64,16,256]{2,1,0:T(8,128)(2,1)S(1)} %copy-done.5, bf16[8,2048,128]{2,1,0:T(8,128)(2,1)S(1)} %bitcast.34, bf16[256,2048]{1,0:T(8,128)(2,1)S(1)} %maximum_bitcast_fusion.2.lag_ref), custom_call_target="tpu_custom_call" | custom-call | flops 2147483648 | bytes 6291456 | tf_op jit(solution)/shard_map/pallas_call | solution.py:86
  202.4 2.2 copy-done.3
  204.6 11.3 %shard_map.49 = f32[16,64,128]{2,1,0:T(8,128)} custom-call(bf16[64,16,256]{2,1,0:T(8,128)(2,1)S(1)} %copy-done.4, bf16[8,2048,128]{2,1,0:T(8,128)(2,1)S(1)} %bitcast.35, bf16[256,2048]{1,0:T(8,128)(2,1)S(1)} %maximum_bitcast_fusion.2.lag_ref), custom_call_target="tpu_custom_call" | custom-call | flops 2147483648 | bytes 6291456 | tf_op jit(solution)/shard_map/pallas_call | solution.py:86
  216.0 6.8 %reduce-scatter.9.cloned.1.call-done = f32[8,64,128]{2,1,0:T(8,128)} async-done(((f32[16,64,128]{2,1,0:T(8,128)}), f32[8,64,128]{2,1,0:T(8,128)}) %reduce-scatter.9.cloned.1.call-update) | async-done | bytes 262160 | tf_op jit(solution)/shard_map/reduce_scatter | solution.py:129
  222.8 16.7 %reduce-scatter.11.cloned.1.call-done = f32[8,64,128]{2,1,0:T(8,128)} async-done(((f32[16,64,128]{2,1,0:T(8,128)}), f32[8,64,128]{2,1,0:T(8,128)}) %reduce-scatter.11.cloned.1.call-update) | async-done | bytes 262160 | tf_op jit(solution)/shard_map/reduce_scatter | solution.py:129
  239.5 2.3 maximum_select_fusion
  (32 shorter events, 0.4 us)
Async XLA Ops:
  6.5 153.7 %all-reduce.3.cloned.1.call-start = ((), (), s32[]{:S(2)}) async-start(), calls=%async_computation.8 | async-start | bytes 4194304 | tf_op jit(solution)/shard_map/psum | solution.py:18
  37.4 6.9 %copy-start.10 = (s32[4]{0:T(128)S(1)}, s32[4]{0:T(128)}, u32[]{:S(2)}) copy-start(s32[4]{0:T(128)} %param.5) | copy-start | bytes 52
  55.1 4.6 %copy-start.8 = (bf16[4,64,2,2048]{3,2,1,0:T(2,128)(2,1)S(1)}, bf16[4,64,2,2048]{3,2,1,0:T(2,128)(2,1)}, u32[]{:S(2)}) copy-start(bf16[4,64,2,2048]{3,2,1,0:T(2,128)(2,1)} %param.4) | copy-start | bytes 6291460
  59.6 156.3 %reduce-scatter.5.cloned.1.call-start = ((), (), s32[]{:S(2)}) async-start(), calls=%async_computation.4 | async-start | bytes 786432 | tf_op jit(solution)/shard_map/reduce_scatter | solution.py:129
  160.2 2.2 copy-start
  162.4 1.0 copy-start.7
  163.5 11.6 %copy-start.6 = (bf16[64,16,256]{2,1,0:T(8,128)(2,1)S(1)}, bf16[64,16,256]{2,1,0:T(8,128)(2,1)}, u32[]{:S(2)}) copy-start(bf16[64,16,256]{2,1,0:T(8,128)(2,1)} %get-tuple-element.7.src_ref) | copy-start | bytes 1572868
  174.8 41.2 %reduce-scatter.7.cloned.1.call-start = ((), (), s32[]{:S(2)}) async-start(), calls=%async_computation.5 | async-start | bytes 786432 | tf_op jit(solution)/shard_map/reduce_scatter | solution.py:129
  175.1 2.2 copy-start.1
  177.3 11.4 %copy-start.5 = (bf16[64,16,256]{2,1,0:T(8,128)(2,1)S(1)}, bf16[64,16,256]{2,1,0:T(8,128)(2,1)}, u32[]{:S(2)}) copy-start(bf16[64,16,256]{2,1,0:T(8,128)(2,1)} %get-tuple-element.6.src_ref) | copy-start | bytes 1572868
  188.6 34.1 %reduce-scatter.9.cloned.1.call-start = ((), (), s32[]{:S(2)}) async-start(), calls=%async_computation.6 | async-start | bytes 786432 | tf_op jit(solution)/shard_map/reduce_scatter | solution.py:129
  188.7 2.2 copy-start.2
  190.9 11.4 %copy-start.4 = (bf16[64,16,256]{2,1,0:T(8,128)(2,1)S(1)}, bf16[64,16,256]{2,1,0:T(8,128)(2,1)}, u32[]{:S(2)}) copy-start(bf16[64,16,256]{2,1,0:T(8,128)(2,1)} %get-tuple-element.5.src_ref) | copy-start | bytes 1572868
  202.3 37.2 %reduce-scatter.11.cloned.1.call-start = ((), (), s32[]{:S(2)}) async-start(), calls=%async_computation.7 | async-start | bytes 786432 | tf_op jit(solution)/shard_map/reduce_scatter | solution.py:129
  202.3 2.2 copy-start.3
  204.6 34.9 %copy-start.9 = (s32[4,8,64]{2,1,0:T(8,128)S(1)}, s32[4,8,64]{2,1,0:T(8,128)}, u32[]{:S(2)}) copy-start(s32[4,8,64]{2,1,0:T(8,128)} %param.7) | copy-start | bytes 24580
Sparse Core Ops, SparseCore 0:
  59.8 100.4 all-reduce.2
  175.0 14.1 reduce-scatter.4
  191.4 14.5 reduce-scatter.6
  208.2 14.5 reduce-scatter.8
  224.9 14.5 reduce-scatter.10

commit v2 on v1

--- a/solution.py
+++ b/solution.py
@@ -2,6 +2,7 @@
 
 import jax
 import jax.numpy as jnp
+import numpy as np
 from jax import lax
 from jax.experimental import pallas as pl
 from jax.experimental.pallas import tpu as pltpu
@@ -13,21 +14,254 @@
 LANES = 128
 
 
-def from_root(value, axis, source):
-    kept = jnp.where(lax.axis_index(axis) == source, value, 0).astype(value.dtype)
-    return lax.psum(kept, axis)
-
-
-def lag_table(bin_count, lag_count, window_count):
-    bins = jnp.arange(bin_count, dtype=jnp.int32)[:, None]
-    offsets = jnp.arange(lag_count, dtype=jnp.int32)[None, :] - lag_count // 2
-    phase = (bins * offsets % (2 * bin_count)).astype(jnp.float32) * (jnp.pi / bin_count)
-    weight = jnp.where(bins == 0, 1.0, 2.0).astype(jnp.float32) / jnp.sqrt(
-        jnp.float32(2.0 * bin_count * window_count)
+def lag_rows(bin_count, lag_count, window_count):
+    bins = np.arange(bin_count, dtype=np.int64)[None, :]
+    offsets = np.arange(lag_count, dtype=np.int64)[:, None] - lag_count // 2
+    phase = (bins * offsets % (2 * bin_count)) * (np.pi / bin_count)
+    weight = np.where(bins == 0, 1.0, 2.0) / np.sqrt(2.0 * bin_count * window_count)
+    rows = np.concatenate([weight * np.cos(phase), -weight * np.sin(phase)], 0)
+    return rows.astype(np.float32).astype(jnp.bfloat16)
+
+
+def prepare_kernel(blocks_ref, spectra_ref, laid_ref, recv_ref, *, run):
+    windows, _, _, bins = spectra_ref.shape
+    steps, _, sources, _ = laid_ref.shape
+    terms = 2 * windows
+    block = lax.broadcasted_iota(jnp.int32, (sources, LANES), 1) // run
+
+    def chunk_step(q, carry):
+        at = pl.ds(pl.multiple_of(q * LANES, LANES), LANES)
+        for w in range(windows):
+            real = spectra_ref[w, 0, :, at].astype(jnp.float32)
+            imag = spectra_ref[w, 1, :, at].astype(jnp.float32)
+            recv_ref[2 * w, at, :] = jnp.concatenate([real, -imag], 0).T.astype(jnp.bfloat16)
+            recv_ref[2 * w + 1, at, :] = jnp.concatenate([imag, real], 0).T.astype(jnp.bfloat16)
+        for step in range(steps):
+            first = pl.ds(pl.multiple_of(blocks_ref[step] * sources, sources), sources)
+            tiles = [
+                spectra_ref[i // 2, i % 2, first, at].astype(jnp.float32) for i in range(terms)
+            ]
+            gap = terms // 2
+            while gap:
+                high = (block // gap) % 2 == 1
+                for i in range(terms):
+                    if (i // gap) % 2 == 0:
+                        low_tile, high_tile = tiles[i], tiles[i + gap]
+                        tiles[i] = jnp.where(
+                            high, pltpu.roll(high_tile, gap * run, 1), low_tile
+                        )
+                        tiles[i + gap] = jnp.where(
+                            high, high_tile, pltpu.roll(low_tile, LANES - gap * run, 1)
+                        )
+                gap //= 2
+            for i in range(terms // 2):
+                laid_ref[step, q * (terms // 2) + i] = jnp.concatenate(
+                    tiles[2 * i : 2 * i + 2], 1
+                ).astype(jnp.bfloat16)
+        return carry
+
+    lax.fori_loop(0, bins // LANES, chunk_step, 0)
+
+
+def prepare(spectra, blocks, steps, sources, run):
+    windows, channels, _, bins = spectra.shape
+    return pl.pallas_call(
+        functools.partial(prepare_kernel, run=run),
+        out_shape=(
+            jax.ShapeDtypeStruct((steps, bins // (2 * run), sources, 2 * LANES), spectra.dtype),
+            jax.ShapeDtypeStruct((2 * windows, bins, 2 * channels), spectra.dtype),
+        ),
+        in_specs=[
+            pl.BlockSpec(memory_space=pltpu.SMEM),
+            pl.BlockSpec(memory_space=pltpu.VMEM),
+        ],
+        out_specs=(pl.BlockSpec(memory_space=pltpu.VMEM), pl.BlockSpec(memory_space=pltpu.VMEM)),
+        compiler_params=pltpu.CompilerParams(vmem_limit_bytes=32 << 20),
+    )(blocks, spectra.transpose(0, 2, 1, 3))
+
+
+def spread_kernel(
+    owners_ref, own_ref, out_ref,
+    from_core, half, from_cross, quarter, from_low, from_high, to_high, to_low,
+    core_send, core_recv, cross_send, cross_recv, up_send, up_recv,
+    down_send, down_recv, share_send, share_recv, last_send, last_recv,
+    *, length,
+):
+    steps = own_ref.shape[0]
+    me = lax.axis_index("chan")
+    line, cross, core = me // 4, (me // 2) % 2, me % 2
+    core_peer = me + 1 - 2 * core
+    cross_peer = me + 2 - 4 * cross
+    mine = 2 * core + cross
+    theirs = 2 * core + 1 - cross
+    has_low, has_high = line > 0, line < length - 1
+
+    def remote(src, dst, send, recv, peer):
+        return pltpu.make_async_remote_copy(
+            src_ref=src, dst_ref=dst, send_sem=send, recv_sem=recv,
+            device_id={"chan": peer}, device_id_type=pl.DeviceIdType.MESH,
+        )
+
+    def to_core(s):
+        part = own_ref.at[s, pl.ds(2 * (1 - core), 2)]
+        return remote(part, from_core.at[s], core_send.at[s], core_recv.at[s], core_peer)
+
+    def to_cross(s):
+        return remote(
+            half.at[s, 1 - cross], from_cross.at[s], cross_send.at[s], cross_recv.at[s],
+            cross_peer,
+        )
+
+    def go_up(s):
+        return remote(to_high.at[s], from_low.at[s], up_send.at[s], up_recv.at[s], me + 4)
+
+    def go_down(s):
+        return remote(to_low.at[s], from_high.at[s], down_send.at[s], down_recv.at[s], me - 4)
+
+    def share(s):
+        ref = out_ref.at[s, mine]
+        return remote(ref, ref, share_send.at[s], share_recv.at[s], cross_peer)
+
+    def last(s, which, index):
+        ref = out_ref.at[s, index]
+        return remote(ref, ref, last_send.at[s, which], last_recv.at[s, which], core_peer)
+
+    barrier = pltpu.get_barrier_semaphore()
+
+    def greet(peer):
+        pl.semaphore_signal(
+            barrier, inc=1, device_id={"chan": peer}, device_id_type=pl.DeviceIdType.MESH
+        )
+
+    greet(core_peer)
+    greet(cross_peer)
+
+    @pl.when(has_low)
+    def _():
+        greet(me - 4)
+
+    @pl.when(has_high)
+    def _():
+        greet(me + 4)
+
+    pl.semaphore_wait(
+        barrier, 2 + jnp.where(has_low, 1, 0) + jnp.where(has_high, 1, 0)
     )
-    return jnp.concatenate([weight * jnp.cos(phase), -weight * jnp.sin(phase)], 1).astype(
-        jnp.bfloat16
-    )
+
+    @pl.loop(0, steps)
+    def _(s):
+        to_core(s).start()
+
+    @pl.loop(0, steps)
+    def _(s):
+        to_core(s).wait_recv()
+        half[s] = lax.select(owners_ref[s] == me, own_ref[s, pl.ds(2 * core, 2)], from_core[s])
+        to_cross(s).start()
+
+    @pl.loop(0, steps)
+    def _(s):
+        to_cross(s).wait_recv()
+        value = lax.select((owners_ref[s] // 2) % 2 == cross, half[s, cross], from_cross[s])
+        quarter[s] = value
+
+        @pl.when(line == 0)
+        def _():
+            to_high[s] = value
+            go_up(s).start()
+
+        @pl.when(line == length - 1)
+        def _():
+            to_low[s] = value
+            go_down(s).start()
+
+    def low_side(s):
+        @pl.when(has_low)
+        def _():
+            go_up(s).wait_recv()
+            to_high[s] = lax.select(owners_ref[s] // 4 == line, quarter[s], from_low[s])
+
+            @pl.when(has_high)
+            def _():
+                go_up(s).start()
+
+    def high_side(s):
+        @pl.when(has_high)
+        def _():
+            go_down(s).wait_recv()
+            to_low[s] = lax.select(owners_ref[s] // 4 == line, quarter[s], from_high[s])
+
+            @pl.when(has_low)
+            def _():
+                go_down(s).start()
+
+    def finish(s):
+        share(s).wait_recv()
+        last(s, 1, theirs).start()
+
+    @pl.loop(0, steps)
+    def _(s):
+        @pl.when(line < length // 2)
+        def _():
+            low_side(s)
+            high_side(s)
+
+        @pl.when(line >= length // 2)
+        def _():
+            high_side(s)
+            low_side(s)
+
+        out_ref[s, mine] = lax.select(owners_ref[s] // 4 <= line, to_high[s], to_low[s])
+        share(s).start()
+        last(s, 0, mine).start()
+
+        @pl.when(s > 0)
+        def _():
+            finish(s - 1)
+
+    finish(steps - 1)
+
+    @pl.loop(0, steps)
+    def _(s):
+        to_core(s).wait_send()
+        to_cross(s).wait_send()
+        share(s).wait_send()
+        for which in range(2):
+            last(s, which, mine).wait()
+
+        @pl.when(has_high)
+        def _():
+            go_up(s).wait_send()
+
+        @pl.when(has_low)
+        def _():
+            go_down(s).wait_send()
+
+
+def spread(laid, owners):
+    steps, groups, sources, width = laid.shape
+    rows = groups * sources // 4
+    dtype = laid.dtype
+    piece = (steps, rows, width)
+    out = pl.pallas_call(
+        functools.partial(spread_kernel, length=lax.axis_size("chan") // 4),
+        out_shape=jax.ShapeDtypeStruct((steps, 4, rows, width), dtype),
+        in_specs=[
+            pl.BlockSpec(memory_space=pltpu.SMEM),
+            pl.BlockSpec(memory_space=pltpu.VMEM),
+        ],
+        out_specs=pl.BlockSpec(memory_space=pltpu.VMEM),
+        scratch_shapes=[
+            pltpu.VMEM((steps, 2, rows, width), dtype),
+            pltpu.VMEM((steps, 2, rows, width), dtype),
+        ]
+        + [pltpu.VMEM(piece, dtype)] * 6
+        + [pltpu.SemaphoreType.DMA((steps,))] * 10
+        + [pltpu.SemaphoreType.DMA((steps, 2))] * 2,
+        compiler_params=pltpu.CompilerParams(
+            collective_id=0, has_side_effects=True, vmem_limit_bytes=32 << 20
+        ),
+    )(owners, laid.reshape(steps, 4, rows, width))
+    return out.reshape(steps, groups, sources, width)
 
 
 def step_kernel(src_ref, recv_ref, lag_ref, out_ref, cross, *, terms, run, receivers):
@@ -102,30 +336,19 @@
 def body(spectra, owners, blocks, max_lag):
     window_count, channel_count, _, bin_count = spectra.shape
     group_count = lax.axis_size("win")
-    terms = 2 * window_count
-    run = LANES // terms
-    groups = bin_count // (2 * run)
-    lag_rows = lag_table(bin_count, LAGS, window_count * group_count).T
-
-    laid = spectra.reshape(window_count, channel_count, 2, groups, 2, run)
-    laid = laid.transpose(3, 1, 4, 0, 2, 5).reshape(groups, channel_count, 2 * LANES)
-
-    turned = spectra.transpose(0, 2, 3, 1)
-    real, imag = turned[:, 0], turned[:, 1]
-    received = jnp.stack(
-        [jnp.concatenate([real, -imag], -1), jnp.concatenate([imag, real], -1)], 1
-    ).reshape(terms, bin_count, 2 * channel_count)
-
-    def pick(step_index):
-        return lax.dynamic_slice_in_dim(laid, blocks[step_index] * SRC, SRC, 1)
-
-    def fetch(step_index):
-        return from_root(pick(step_index), "chan", owners[step_index])
-
-    incoming = [fetch(step_index) for step_index in range(STEPS)]
+    run = LANES // (2 * window_count)
+    table = jnp.asarray(lag_rows(bin_count, LAGS, window_count * group_count))
+    laid, received = prepare(spectra, blocks, STEPS, SRC, run)
+    incoming = spread(laid, owners)
 
     def stack_step(source_all):
-        made = correlate(source_all, received, lag_rows, channel_count, run)
+        made = correlate(source_all, received, table, channel_count, run)
+        if group_count == 2:
+            kept = SRC // 2
+            place = lax.axis_index("win")
+            sent = lax.dynamic_slice_in_dim(made, (1 - place) * kept, kept, 0)
+            other = lax.ppermute(sent, "win", [(0, 1), (1, 0)])
+            return lax.dynamic_slice_in_dim(made, place * kept, kept, 0) + other
         return lax.psum_scatter(made, "win", scatter_dimension=0, tiled=True)
 
     stacked = jnp.stack([stack_step(incoming[step_index]) for step_index in range(STEPS)])

time: 249 us -> 119 us (0.48)
  waiting for transfers between devices: 109 us -> 4.23 us
  local copies, waits for them, and re-layouts: 61.9 us -> 8.1 us
  Pallas kernels: 45.4 us -> 98.1 us
  between operations: 18.4 us -> 0.18 us
  other arithmetic: 13.2 us -> 4.23 us
  starting transfers between devices: 0.35 us -> 4.33 us
    psum x1 -> x0, waiting for transfers between devices: 85.4 us -> none  [from_root(): return lax.psum(kept, axis)]
    pallas_call x0 -> x2, Pallas kernels: none -> 55.9 us  [the longest x1 46.7 us: spread(): pl.pallas_call(functools.partial(spread_kernel, length=lax.axis_size('cha...]
    unnamed x28 -> x13, local copies, waits for them, and re-layouts: 33.5 us -> 7.86 us
    reduce_scatter x4 -> x0, waiting for transfers between devices: 23.5 us -> none  [stack_step(): return lax.psum_scatter(made, 'win', scatter_dimension=0, tiled=True)]
    dynamic_slice x1 -> x4, local copies, waits for them, and re-layouts: 14.6 us -> 0.11 us  [stack_step(): sent = lax.dynamic_slice_in_dim(made, (1 - place) * kept, kept, 0)]
    another operation x1 -> x0, local copies, waits for them, and re-layouts: 6.25 us -> none  [body(): jnp.stack([jnp.concatenate([real, -imag], -1), jnp.concatenate([imag, rea...]
    transpose x1 -> x0, local copies, waits for them, and re-layouts: 5.42 us -> none  [body(): laid.transpose(3, 1, 4, 0, 2, 5).reshape(groups, channel_count, 2 * LANES)]
    another operation x3 -> x4, other arithmetic: 7.61 us -> 2.98 us  [body(): jnp.stack([stack_step(incoming[step_index]) for step_index in range(STEPS)])]
  transfers between devices with their start and end apart: 5 -> 4, of which waited for: 3 -> 1; matrix products, arithmetic and copies ran while one was open for 6% -> 3% of each run, Pallas kernels for 14% -> 27%
where the time goes in v2:
time: 119 us
  Pallas kernels  98.1 us (82%)
  local copies, waits for them, and re-layouts  8.1 us (7%)
  starting transfers between devices  4.33 us (4%)
  other arithmetic  4.23 us (4%)
  waiting for transfers between devices  4.23 us (4%)
    pallas_call x1, Pallas kernels, spread(): pl.pallas_call(functools.partial(spread_kernel, length=lax.axis_size('cha...  46.7 us
    pallas_call x4, Pallas kernels, correlate(): pl.pallas_call(functools.partial(step_kernel, terms=terms, run=run, recei...  42.2 us
    pallas_call x1, Pallas kernels, prepare(): pl.pallas_call(functools.partial(prepare_kernel, run=run), out_shape=(jax...  9.2 us
    unnamed x13, local copies, waits for them, and re-layouts  7.86 us
    ppermute x4, starting transfers between devices, stack_step(): other = lax.ppermute(sent, 'win', [(0, 1), (1, 0)])  4.33 us
    ppermute x4, waiting for transfers between devices, stack_step(): other = lax.ppermute(sent, 'win', [(0, 1), (1, 0)])  4.23 us
    another operation x4, other arithmetic, body(): jnp.stack([stack_step(incoming[step_index]) for step_index in range(STEPS)])  2.98 us
  transfers between devices with their start and end apart: 4, of which 1 were waited for; matrix products, arithmetic and copies ran while one was open for 3% of the time, Pallas kernels for 27%

profile of v2, /device:TPU:0, one launch (start us, length us, event | category | flops | bytes accessed | tf_op | source)
XLA Modules:
  0.0 119.1 jit_solution(476756585004388170)
XLA Ops:
  0.0 0.0 copy-start
  0.0 2.5 %copy.8 = bf16[4,64,2,2048]{3,1,2,0:T(8,128)(2,1)S(1)} copy(bf16[4,64,2,2048]{3,2,1,0:T(2,128)(2,1)} %param.5) | data formatting | bytes 4194304 | tf_op args[0]
  2.5 0.0 copy-start.1
  2.5 0.0 copy-done
  2.5 9.2 %shard_map.55 = (bf16[4,64,16,256]{3,2,1,0:T(8,128)(2,1)S(1)}, bf16[8,2048,128]{2,1,0:T(8,128)(2,1)S(1)}) custom-call(s32[4]{0:T(128)S(1)} %copy-done, bf16[4,2,64,2048]{3,2,1,0:T(8,128)(2,1)S(1)} %bitcast.16), custom_call_target="tpu_custom_call" | custom-call | tf_op jit(solution)/shard_map/pallas_call | solution.py:68
  11.7 0.0 copy-start.2
  11.7 1.9 %copy-done.2 = bf16[8,2048,128]{2,1,0:T(8,128)(2,1)} copy-done((bf16[8,2048,128]{2,1,0:T(8,128)(2,1)}, bf16[8,2048,128]{2,1,0:T(8,128)(2,1)S(1)}, u32[]{:S(2)}) %copy-start.2) | copy-done | bytes 4194328
  13.7 0.0 copy-done.1
  13.7 46.7 %shard_map.56 = bf16[4,4,256,256]{3,2,1,0:T(8,128)(2,1)S(1)} custom-call(s32[4]{0:T(128)S(1)} %copy-done.1, bf16[4,4,256,256]{3,2,1,0:T(8,128)(2,1)S(1)} %bitcast.17), custom_call_target="tpu_custom_call" | custom-call | tf_op jit(solution)/shard_map/pallas_call | solution.py:245
  60.4 0.1 fusion
  60.5 0.0 copy-start.3
  60.5 2.2 %copy-done.3 = bf16[8,2048,128]{2,1,0:T(8,128)(2,1)S(1)} copy-done((bf16[8,2048,128]{2,1,0:T(8,128)(2,1)S(1)}, bf16[8,2048,128]{2,1,0:T(8,128)(2,1)}, u32[]{:S(2)}) %copy-start.3) | copy-done | bytes 4194328
  62.7 0.0 copy-start.4
  62.7 1.2 %copy-done.4 = bf16[256,2048]{1,0:T(8,128)(2,1)S(1)} copy-done((bf16[256,2048]{1,0:T(8,128)(2,1)S(1)}, bf16[256,2048]{1,0:T(8,128)(2,1)}, u32[]{:S(2)}) %copy-start.4) | copy-done | bytes 1048600
  63.9 10.6 %shard_map.60 = f32[16,64,128]{2,1,0:T(8,128)S(1)} custom-call(bf16[64,16,256]{2,1,0:T(8,128)(2,1)S(1)} %bitcast.21, bf16[8,2048,128]{2,1,0:T(8,128)(2,1)S(1)} %copy-done.3, bf16[256,2048]{1,0:T(8,128)(2,1)S(1)} %copy-done.4), custom_call_target="tpu_custom_call" | custom-call | flops 2147483648 | bytes 6291456 | tf_op jit(solution)/shard_map/pallas_call | solution.py:320
  74.5 1.6 %collective-permute-start.3 = (f32[8,64,128]{2,1,0:T(8,128)S(1)}, f32[8,64,128]{2,1,0:T(8,128)}, u32[]{:S(2)}, u32[]{:S(2)}) collective-permute-start(f32[8,64,128]{2,1,0:T(8,128)S(1)} %constant_dynamic-slice_fusion), channel_id=1, source_target_pairs={{0,1},{1,0},{2,3},{3,2},{4,5},{5,4},{6,7},{7,6},{8,9},{9,8},{10,11... | collective-permute-start | bytes 786440 | tf_op jit(solution)/shard_map/ppermute | solution.py:350
  76.1 10.6 %shard_map.59 = f32[16,64,128]{2,1,0:T(8,128)S(1)} custom-call(bf16[64,16,256]{2,1,0:T(8,128)(2,1)S(1)} %bitcast.20, bf16[8,2048,128]{2,1,0:T(8,128)(2,1)S(1)} %copy-done.3, bf16[256,2048]{1,0:T(8,128)(2,1)S(1)} %copy-done.4), custom_call_target="tpu_custom_call" | custom-call | flops 2147483648 | bytes 6291456 | tf_op jit(solution)/shard_map/pallas_call | solution.py:320
  86.7 0.6 collective-permute-start.2
  87.3 10.6 %shard_map.58 = f32[16,64,128]{2,1,0:T(8,128)S(1)} custom-call(bf16[64,16,256]{2,1,0:T(8,128)(2,1)S(1)} %bitcast.19, bf16[8,2048,128]{2,1,0:T(8,128)(2,1)S(1)} %copy-done.3, bf16[256,2048]{1,0:T(8,128)(2,1)S(1)} %copy-done.4), custom_call_target="tpu_custom_call" | custom-call | flops 2147483648 | bytes 6291456 | tf_op jit(solution)/shard_map/pallas_call | solution.py:320
  97.9 1.6 %collective-permute-start.1 = (f32[8,64,128]{2,1,0:T(8,128)S(1)}, f32[8,64,128]{2,1,0:T(8,128)}, u32[]{:S(2)}, u32[]{:S(2)}) collective-permute-start(f32[8,64,128]{2,1,0:T(8,128)S(1)} %constant_dynamic-slice_fusion.2), channel_id=1, source_target_pairs={{0,1},{1,0},{2,3},{3,2},{4,5},{5,4},{6,7},{7,6},{8,9},{9,8},{10,11... | collective-permute-start | bytes 786440 | tf_op jit(solution)/shard_map/ppermute | solution.py:350
  99.5 10.6 %shard_map.57 = f32[16,64,128]{2,1,0:T(8,128)S(1)} custom-call(bf16[64,16,256]{2,1,0:T(8,128)(2,1)S(1)} %bitcast.18, bf16[8,2048,128]{2,1,0:T(8,128)(2,1)S(1)} %copy-done.3, bf16[256,2048]{1,0:T(8,128)(2,1)S(1)} %copy-done.4), custom_call_target="tpu_custom_call" | custom-call | flops 2147483648 | bytes 6291456 | tf_op jit(solution)/shard_map/pallas_call | solution.py:320
  110.0 0.0 copy-start.5
  110.1 0.6 collective-permute-start
  110.6 0.0 collective-permute-done.3
  110.6 1.0 add_bitcast_fusion
  111.6 0.0 collective-permute-done.2
  111.6 1.0 add_bitcast_fusion.1
  112.6 0.0 collective-permute-done.1
  112.6 1.0 add_bitcast_fusion.2
  113.6 4.2 %collective-permute-done = f32[8,64,128]{2,1,0:T(8,128)S(1)} collective-permute-done((f32[8,64,128]{2,1,0:T(8,128)S(1)}, f32[8,64,128]{2,1,0:T(8,128)S(1)}, u32[]{:S(2)}, u32[]{:S(2)}) %collective-permute-start) | collective-permute-done | bytes 262176 | tf_op jit(solution)/shard_map/ppermute | solution.py:350
  117.9 0.0 copy-done.5
  117.9 1.2 %maximum_select_fusion = f32[4,8,64,128]{3,2,1,0:T(8,128)} fusion(f32[1,8,64,128]{3,2,1,0:T(8,128)S(1)} %add_bitcast_fusion, f32[1,8,64,128]{3,2,1,0:T(8,128)S(1)} %add_bitcast_fusion.1, f32[1,8,64,128]{3,2,1,0:T(8,128)S(1)} %add_bitcast_fusion.2, f32[1,8,64,128]{3,2,1,0:T(8,128)S(1)} %add_bitcast_fusion.3, s32[4,8,64]{2,1,0:T(8,128)S(1)} %copy-done.5, ...), kind=kLoop, calls=%fused_computation.1 | loop fusion | flops 1310720 | bytes 2105856 | tf_op jit(solution)/shard_map/jit(_where)/select_n | solution.py:357
  (6 shorter events, 0.1 us)
Async XLA Ops:
  0.0 2.5 %copy-start = (s32[4]{0:T(128)S(1)}, s32[4]{0:T(128)}, u32[]{:S(2)}) copy-start(s32[4]{0:T(128)} %blocks_ref.1) | copy-start | bytes 52
  2.5 11.2 %copy-start.1 = (s32[4]{0:T(128)S(1)}, s32[4]{0:T(128)}, u32[]{:S(2)}) copy-start(s32[4]{0:T(128)} %owners_ref.1) | copy-start | bytes 52
  11.7 2.0 %copy-start.2 = (bf16[8,2048,128]{2,1,0:T(8,128)(2,1)}, bf16[8,2048,128]{2,1,0:T(8,128)(2,1)S(1)}, u32[]{:S(2)}) copy-start(bf16[8,2048,128]{2,1,0:T(8,128)(2,1)S(1)} %get-tuple-element.8.recv_ref) | copy-start | bytes 12582916
  60.5 2.2 %copy-start.3 = (bf16[8,2048,128]{2,1,0:T(8,128)(2,1)S(1)}, bf16[8,2048,128]{2,1,0:T(8,128)(2,1)}, u32[]{:S(2)}) copy-start(bf16[8,2048,128]{2,1,0:T(8,128)(2,1)} %copy-done.2) | copy-start | bytes 12582916
  62.7 1.2 %copy-start.4 = (bf16[256,2048]{1,0:T(8,128)(2,1)S(1)}, bf16[256,2048]{1,0:T(8,128)(2,1)}, u32[]{:S(2)}) copy-start(bf16[256,2048]{1,0:T(8,128)(2,1)} %constant.19.clone.lag_ref) | copy-start | bytes 3145732
  74.5 36.1 %collective-permute-start.3 = (f32[8,64,128]{2,1,0:T(8,128)S(1)}, f32[8,64,128]{2,1,0:T(8,128)}, u32[]{:S(2)}, u32[]{:S(2)}) collective-permute-start(f32[8,64,128]{2,1,0:T(8,128)S(1)} %constant_dynamic-slice_fusion), channel_id=1, source_target_pairs={{0,1},{1,0},{2,3},{3,2},{4,5},{5,4},{6,7},{7,6},{8,9},{9,8},{10,11... | collective-permute-start | bytes 786440 | tf_op jit(solution)/shard_map/ppermute | solution.py:350
  86.7 24.9 %collective-permute-start.2 = (f32[8,64,128]{2,1,0:T(8,128)S(1)}, f32[8,64,128]{2,1,0:T(8,128)}, u32[]{:S(2)}, u32[]{:S(2)}) collective-permute-start(f32[8,64,128]{2,1,0:T(8,128)S(1)} %constant_dynamic-slice_fusion.1), channel_id=1, source_target_pairs={{0,1},{1,0},{2,3},{3,2},{4,5},{5,4},{6,7},{7,6},{8,9},{9,8},{10,11... | collective-permute-start | bytes 786440 | tf_op jit(solution)/shard_map/ppermute | solution.py:350
  97.9 14.8 %collective-permute-start.1 = (f32[8,64,128]{2,1,0:T(8,128)S(1)}, f32[8,64,128]{2,1,0:T(8,128)}, u32[]{:S(2)}, u32[]{:S(2)}) collective-permute-start(f32[8,64,128]{2,1,0:T(8,128)S(1)} %constant_dynamic-slice_fusion.2), channel_id=1, source_target_pairs={{0,1},{1,0},{2,3},{3,2},{4,5},{5,4},{6,7},{7,6},{8,9},{9,8},{10,11... | collective-permute-start | bytes 786440 | tf_op jit(solution)/shard_map/ppermute | solution.py:350
  110.0 7.9 %copy-start.5 = (s32[4,8,64]{2,1,0:T(8,128)S(1)}, s32[4,8,64]{2,1,0:T(8,128)}, u32[]{:S(2)}) copy-start(s32[4,8,64]{2,1,0:T(8,128)} %param.8) | copy-start | bytes 24580
  110.1 7.8 %collective-permute-start = (f32[8,64,128]{2,1,0:T(8,128)S(1)}, f32[8,64,128]{2,1,0:T(8,128)S(1)}, u32[]{:S(2)}, u32[]{:S(2)}) collective-permute-start(f32[8,64,128]{2,1,0:T(8,128)S(1)} %constant_dynamic-slice_fusion.3), channel_id=1, source_target_pairs={{0,1},{1,0},{2,3},{3,2},{4,5},{5,4},{6,7},{7,6},{8,9},{9,8},{10,11... | collective-permute-start | bytes 786440 | tf_op jit(solution)/shard_map/ppermute | solution.py:350

commit v3 on v2

v3 whole, which is shorter than its diff:
```python
import functools

import jax
import jax.numpy as jnp
import numpy as np
from jax import lax
from jax.experimental import pallas as pl
from jax.experimental.pallas import tpu as pltpu
from jax.sharding import PartitionSpec as P

SRC = 16
STEPS = 4
LAGS = 128
LANES = 128


def lag_rows(bin_count, lag_count, window_count):
    bins = np.arange(bin_count, dtype=np.int64)[None, :]
    offsets = np.arange(lag_count, dtype=np.int64)[:, None] - lag_count // 2
    phase = (bins * offsets % (2 * bin_count)) * (np.pi / bin_count)
    weight = np.where(bins == 0, 1.0, 2.0) / np.sqrt(2.0 * bin_count * window_count)
    rows = np.concatenate([weight * np.cos(phase), -weight * np.sin(phase)], 0)
    return rows.astype(np.float32).astype(jnp.bfloat16)


def prepare_kernel(blocks_ref, spectra_ref, laid_ref, *, run):
    terms = 2 * spectra_ref.shape[0]
    bins = spectra_ref.shape[3]
    steps, _, sources, _ = laid_ref.shape
    block = lax.broadcasted_iota(jnp.int32, (sources, LANES), 1) // run

    def chunk_step(q, carry):
        at = pl.ds(pl.multiple_of(q * LANES, LANES), LANES)
        for step in range(steps):
            first = pl.ds(pl.multiple_of(blocks_ref[step] * sources, sources), sources)
            tiles = [
                spectra_ref[i // 2, i % 2, first, at].astype(jnp.float32) for i in range(terms)
            ]
            gap = terms // 2
            while gap:
                high = (block // gap) % 2 == 1
                for i in range(terms):
                    if (i // gap) % 2 == 0:
                        low_tile, high_tile = tiles[i], tiles[i + gap]
                        tiles[i] = jnp.where(
                            high, pltpu.roll(high_tile, gap * run, 1), low_tile
                        )
                        tiles[i + gap] = jnp.where(
                            high, high_tile, pltpu.roll(low_tile, LANES - gap * run, 1)
                        )
                gap //= 2
            for i in range(terms // 2):
                laid_ref[step, q * (terms // 2) + i] = jnp.concatenate(
                    tiles[2 * i : 2 * i + 2], 1
                ).astype(jnp.bfloat16)
        return carry

    lax.fori_loop(0, bins // LANES, chunk_step, 0)


def prepare(spectra, blocks, steps, sources, run):
    bins = spectra.shape[3]
    return pl.pallas_call(
        functools.partial(prepare_kernel, run=run),
        out_shape=jax.ShapeDtypeStruct(
            (steps, bins // (2 * run), sources, 2 * LANES), spectra.dtype
        ),
        in_specs=[
            pl.BlockSpec(memory_space=pltpu.SMEM),
            pl.BlockSpec(memory_space=pltpu.VMEM),
        ],
        out_specs=pl.BlockSpec(memory_space=pltpu.VMEM),
        compiler_params=pltpu.CompilerParams(vmem_limit_bytes=16 << 20),
    )(blocks, spectra)


def main_kernel(
    owners_ref, own_ref, spectra_ref, lag_ref, out_ref,
    recv, cross_spectra, made, arrived, got,
    from_core, half, from_cross, quarter, from_low, from_high, to_high, to_low,
    core_send, core_recv, cross_send, cross_recv, up_send, up_recv,
    down_send, down_recv, share_send, share_recv, last_send, last_recv,
    sum_send, sum_recv,
    *, length, members, run,
):
    steps, _, groups, sources, width = own_ref.shape
    windows, _, receivers, bins = spectra_ref.shape
    terms = 2 * windows
    kept = sources // members
    me = lax.axis_index("chan")
    win = lax.axis_index("win")
    line, cross, core = me // 4, (me // 2) % 2, me % 2
    core_peer = me + 1 - 2 * core
    cross_peer = me + 2 - 4 * cross
    mine = 2 * core + cross
    theirs = 2 * core + 1 - cross
    has_low, has_high = line > 0, line < length - 1
    near_low = line < length // 2

    def remote(src, dst, send, recv, peer):
        return pltpu.make_async_remote_copy(
            src_ref=src, dst_ref=dst, send_sem=send, recv_sem=recv,
            device_id={"chan": peer}, device_id_type=pl.DeviceIdType.MESH,
        )

    def to_core(s):
        part = own_ref.at[s, pl.ds(2 * (1 - core), 2)]
        return remote(part, from_core.at[s], core_send.at[s], core_recv.at[s], core_peer)

    def to_cross(s):
        return remote(
            half.at[s, 1 - cross], from_cross.at[s], cross_send.at[s], cross_recv.at[s],
            cross_peer,
        )

    def go_up(s):
        return remote(to_high.at[s], from_low.at[s], up_send.at[s], up_recv.at[s], me + 4)

    def go_down(s):
        return remote(to_low.at[s], from_high.at[s], down_send.at[s], down_recv.at[s], me - 4)

    def share(s):
        ref = got.at[s, mine]
        return remote(ref, ref, share_send.at[s], share_recv.at[s], cross_peer)

    def last(s, which, index):
        ref = got.at[s, index]
        return remote(ref, ref, last_send.at[s, which], last_recv.at[s, which], core_peer)

    def add_up(s, j):
        peer = (win + j) % members
        return pltpu.make_async_remote_copy(
            src_ref=made.at[s, pl.ds(peer * kept, kept)],
            dst_ref=arrived.at[s, j - 1],
            send_sem=sum_send.at[s, j - 1],
            recv_sem=sum_recv.at[s, j - 1],
            device_id={"win": peer},
            device_id_type=pl.DeviceIdType.MESH,
        )

    barrier = pltpu.get_barrier_semaphore()

    def greet(peer):
        pl.semaphore_signal(
            barrier, inc=1, device_id={"chan": peer}, device_id_type=pl.DeviceIdType.MESH
        )

    greet(core_peer)
    greet(cross_peer)
    for j in range(1, members):
        pl.semaphore_signal(
            barrier,
            inc=1,
            device_id={"win": (win + j) % members},
            device_id_type=pl.DeviceIdType.MESH,
        )

    @pl.when(has_low)
    def _():
        greet(me - 4)

    @pl.when(has_high)
    def _():
        greet(me + 4)

    pl.semaphore_wait(
        barrier, 1 + members + jnp.where(has_low, 1, 0) + jnp.where(has_high, 1, 0)
    )

    @pl.loop(0, steps)
    def _(s):
        to_core(s).start()

    @pl.loop(0, steps)
    def _(s):
        to_core(s).wait_recv()
        half[s] = lax.select(owners_ref[s] == me, own_ref[s, pl.ds(2 * core, 2)], from_core[s])
        to_cross(s).start()

    @pl.loop(0, bins // LANES)
    def _(q):
        at = pl.ds(pl.multiple_of(q * LANES, LANES), LANES)
        for w in range(windows):
            real = spectra_ref[w, 0, :, at].astype(jnp.float32)
            imag = spectra_ref[w, 1, :, at].astype(jnp.float32)
            recv[2 * w, at, :] = jnp.concatenate([real, -imag], 0).T.astype(jnp.bfloat16)
            recv[2 * w + 1, at, :] = jnp.concatenate([imag, real], 0).T.astype(jnp.bfloat16)

    lane = lax.broadcasted_iota(jnp.int32, (run, width), 1) % run
    row = lax.broadcasted_iota(jnp.int32, (run, width), 0)
    keep = (lane == row).astype(jnp.float32)
    zero = jnp.zeros((LANES, LANES), jnp.bfloat16)

    def cross_part(s, part):
        def group_step(g, carry):
            base = pl.multiple_of((part * groups + g) * 2 * run, 2 * run)
            first = jnp.concatenate([recv[i, pl.ds(base, run), :] for i in range(terms)], 0)
            second = jnp.concatenate(
                [recv[i, pl.ds(base + run, run), :] for i in range(terms)], 0
            )
            weight = jnp.concatenate(
                [jnp.concatenate([first, zero], 1), jnp.concatenate([zero, second], 1)], 0
            )
            values = got[s, part, g].astype(jnp.float32)
            rows = jnp.concatenate(
                [
                    (jnp.broadcast_to(values[i : i + 1], (run, width)) * keep).astype(
                        jnp.bfloat16
                    )
                    for i in range(sources)
                ],
                0,
            )
            dots = jnp.dot(rows, weight, preferred_element_type=jnp.float32)
            dots = dots.astype(jnp.bfloat16)
            for i in range(sources):
                one = dots[i * run : (i + 1) * run]
                at = slice(i * LANES, (i + 1) * LANES)
                cross_spectra[s, pl.ds(base, run), at] = one[:, :LANES]
                cross_spectra[s, pl.ds(base + run, run), at] = one[:, LANES:]
            return carry

        lax.fori_loop(0, groups, group_step, 0, unroll=2)

    def lag_part(s):
        for pair in range(sources // 2):
            block = jnp.dot(
                lag_ref[...],
                cross_spectra[s, :, pair * 2 * LANES : (pair + 1) * 2 * LANES],
                preferred_element_type=jnp.float32,
            )
            turned = block.T
            lags = turned.shape[1] // 2
            for k in range(2):
                top = k * LANES
                made[s, 2 * pair + k] = (
                    turned[top : top + receivers, :lags]
                    + turned[top + receivers : top + 2 * receivers, lags:]
                )

    def low_side(s):
        @pl.when(has_low)
        def _():
            go_up(s).wait_recv()
            to_high[s] = lax.select(owners_ref[s] // 4 == line, quarter[s], from_low[s])

            @pl.when(has_high)
            def _():
                go_up(s).start()

    def high_side(s):
        @pl.when(has_high)
        def _():
            go_down(s).wait_recv()
            to_low[s] = lax.select(owners_ref[s] // 4 == line, quarter[s], from_high[s])

            @pl.when(has_low)
            def _():
                go_down(s).start()

    def enter(s):
        to_cross(s).wait_recv()
        value = lax.select((owners_ref[s] // 2) % 2 == cross, half[s, cross], from_cross[s])
        quarter[s] = value

        @pl.when(line == 0)
        def _():
            to_high[s] = value
            go_up(s).start()

        @pl.when(line == length - 1)
        def _():
            to_low[s] = value
            go_down(s).start()

    def near_side(s):
        @pl.when(near_low)
        def _():
            low_side(s)

        @pl.when(jnp.logical_not(near_low))
        def _():
            high_side(s)

    def far_side(s):
        @pl.when(near_low)
        def _():
            high_side(s)

        @pl.when(jnp.logical_not(near_low))
        def _():
            low_side(s)

        got[s, mine] = lax.select(owners_ref[s] // 4 <= line, to_high[s], to_low[s])
        share(s).start()
        last(s, 0, mine).start()

    def pass_on(s):
        share(s).wait_recv()
        last(s, 1, theirs).start()

    @pl.loop(0, steps + 2)
    def _(t):
        @pl.when(t < steps)
        def _():
            enter(t)

        @pl.when((t >= 1) & (t <= steps))
        def _():
            near_side(t - 1)

        @pl.when(t >= 2)
        def _():
            far_side(t - 2)

            @pl.when(t >= 3)
            def _():
                pass_on(t - 3)

            cross_part(t - 2, mine)

    pass_on(steps - 1)

    @pl.loop(0, steps)
    def _(s):
        cross_part(s, theirs)
        for which in range(2):
            last(s, which, mine).wait_recv()
        cross_part(s, 2 * (1 - core))
        cross_part(s, 2 * (1 - core) + 1)
        lag_part(s)
        for j in range(1, members):
            add_up(s, j).start()

    @pl.loop(0, steps)
    def _(s):
        to_core(s).wait_send()
        to_cross(s).wait_send()
        share(s).wait_send()
        for which in range(2):
            last(s, which, mine).wait_send()

        @pl.when(has_high)
        def _():
            go_up(s).wait_send()

        @pl.when(has_low)
        def _():
            go_down(s).wait_send()

        total = made[s, pl.ds(win * kept, kept)]
        for j in range(1, members):
            add_up(s, j).wait()
            total += arrived[s, j - 1]
        out_ref[s] = total


def main(laid, spectra, table, owners, run):
    steps, groups, sources, width = laid.shape
    windows, _, receivers, bins = spectra.shape
    members = lax.axis_size("win")
    lags = table.shape[0] // 2
    dtype = laid.dtype
    piece = (groups // 4, sources, width)
    kept = (sources // members, receivers, lags)
    return pl.pallas_call(
        functools.partial(
            main_kernel, length=lax.axis_size("chan") // 4, members=members, run=run
        ),
        out_shape=jax.ShapeDtypeStruct((steps,) + kept, jnp.float32),
        in_specs=[pl.BlockSpec(memory_space=pltpu.SMEM)]
        + [pl.BlockSpec(memory_space=pltpu.VMEM)] * 3,
        out_specs=pl.BlockSpec(memory_space=pltpu.VMEM),
        scratch_shapes=[
            pltpu.VMEM((2 * windows, bins, 2 * receivers), dtype),
            pltpu.VMEM((steps, bins, sources * LANES), dtype),
            pltpu.VMEM((steps, sources, receivers, lags), jnp.float32),
            pltpu.VMEM((steps, members - 1) + kept, jnp.float32),
            pltpu.VMEM((steps, 4) + piece, dtype),
            pltpu.VMEM((steps, 2) + piece, dtype),
            pltpu.VMEM((steps, 2) + piece, dtype),
        ]
        + [pltpu.VMEM((steps,) + piece, dtype)] * 6
        + [pltpu.SemaphoreType.DMA((steps,))] * 10
        + [pltpu.SemaphoreType.DMA((steps, 2))] * 2
        + [pltpu.SemaphoreType.DMA((steps, members - 1))] * 2,
        compiler_params=pltpu.CompilerParams(
            collective_id=0, has_side_effects=True, vmem_limit_bytes=60 << 20
        ),
    )(owners, laid.reshape((steps, 4) + piece), spectra, table)


def body(spectra, owners, blocks, max_lag):
    window_count, _, _, bin_count = spectra.shape
    group_count = lax.axis_size("win")
    run = LANES // (2 * window_count)
    table = jnp.asarray(lag_rows(bin_count, LAGS, window_count * group_count))
    turned = spectra.transpose(0, 2, 1, 3)
    laid = prepare(turned, blocks, STEPS, SRC, run)
    stacked = main(laid, turned, table, owners, run)
    offsets = jnp.abs(jnp.arange(LAGS, dtype=jnp.int32) - LAGS // 2)
    inside = offsets[None, None, None, :] <= max_lag[:, :, :, None]
    return jnp.where(inside, stacked, jnp.float32(0.0))


def solution(mesh):
    return jax.shard_map(
        body,
        mesh=mesh,
        in_specs=(P("win", "chan", None, None), P(), P(), P(None, "win", "chan")),
        out_specs=P(None, "win", "chan", None),
        check_vma=False,
    )
```

time: 119 us -> 97.2 us (0.82)
  Pallas kernels: 98.1 us -> 90.6 us
  starting transfers between devices: 4.33 us -> 0 us
  local copies, waits for them, and re-layouts: 8.1 us -> 3.82 us
  waiting for transfers between devices: 4.23 us -> 0 us
  other arithmetic: 4.23 us -> 2.54 us
    pallas_call x6 -> x2, Pallas kernels: 98.1 us -> 90.6 us  [the longest x1 86 us: main(): pl.pallas_call(functools.partial(main_kernel, length=lax.axis_size('chan'...]
    ppermute x4 -> x0, starting transfers between devices: 4.33 us -> none  [stack_step(): other = lax.ppermute(sent, 'win', [(0, 1), (1, 0)])]
    ppermute x4 -> x0, waiting for transfers between devices: 4.23 us -> none  [stack_step(): other = lax.ppermute(sent, 'win', [(0, 1), (1, 0)])]
    unnamed x13 -> x9, local copies, waits for them, and re-layouts: 7.86 us -> 3.82 us
    another operation x4 -> x0, other arithmetic: 2.98 us -> none  [body(): jnp.stack([stack_step(incoming[step_index]) for step_index in range(STEPS)])]
    select_n x1, other arithmetic: 1.24 us -> 2.53 us  [body(): return jnp.where(inside, stacked, jnp.float32(0.0))]
  transfers between devices with their start and end apart: 4 -> 0, of which waited for: 1 -> 0; matrix products, arithmetic and copies ran while one was open for 3% -> 0% of each run, Pallas kernels for 27% -> 0%
where the time goes in v3:
time: 97.2 us; the launch traced here: 97 us
  Pallas kernels  90.6 us (93%)
  local copies, waits for them, and re-layouts  3.82 us (4%)
  other arithmetic  2.54 us (3%)
    pallas_call x1, Pallas kernels, main(): pl.pallas_call(functools.partial(main_kernel, length=lax.axis_size('chan'...  86 us
    pallas_call x1, Pallas kernels, prepare(): pl.pallas_call(functools.partial(prepare_kernel, run=run), out_shape=jax....  4.64 us
    unnamed x9, local copies, waits for them, and re-layouts  3.82 us
    select_n x1, other arithmetic, body(): return jnp.where(inside, stacked, jnp.float32(0.0))  2.53 us

profile of v3, /device:TPU:0, one launch (start us, length us, event | category | flops | bytes accessed | tf_op | source)
XLA Modules:
  0.0 97.0 jit_solution(3274095221992053533)
XLA Ops:
  0.0 0.0 copy-start.2
  0.0 2.5 %copy.8 = bf16[4,64,2,2048]{3,1,2,0:T(8,128)(2,1)S(1)} copy(bf16[4,64,2,2048]{3,2,1,0:T(2,128)(2,1)} %param.5) | data formatting | bytes 4194304 | tf_op args[0]
  2.5 0.0 copy-start
  2.5 0.0 copy-done.2
  2.5 4.6 %shard_map.55 = bf16[4,64,16,256]{3,2,1,0:T(8,128)(2,1)S(1)} custom-call(s32[4]{0:T(128)S(1)} %copy-done.2, bf16[4,2,64,2048]{3,2,1,0:T(8,128)(2,1)S(1)} %bitcast.4), custom_call_target="tpu_custom_call" | custom-call | tf_op jit(solution)/shard_map/pallas_call | solution.py:63
  7.2 0.0 copy-done
  7.2 0.0 copy-start.1
  7.2 1.3 %copy-done.1 = bf16[4,64,16,256]{3,2,1,0:T(8,128)(2,1)} copy-done((bf16[4,64,16,256]{3,2,1,0:T(8,128)(2,1)}, bf16[4,64,16,256]{3,2,1,0:T(8,128)(2,1)S(1)}, u32[]{:S(2)}) %copy-start.1) | copy-done | bytes 2097176
  8.5 0.0 copy-start.3
  8.5 86.0 %shard_map.56 = f32[4,8,64,128]{3,2,1,0:T(8,128)} custom-call(s32[4]{0:T(128)} %owners_ref.1, bf16[4,4,16,16,256]{4,3,2,1,0:T(8,128)(2,1)} %bitcast.6, bf16[4,2,64,2048]{3,2,1,0:T(8,128)(2,1)} %bitcast.5, bf16[256,2048]{1,0:T(8,128)(2,1)} %constant.7.clone.lag_ref), custom_call_target="tpu_custom_call" | custom-call | tf_op jit(solution)/shard_map/pallas_call | solution.py:366
  94.5 0.0 copy-done.3
  94.5 2.5 %compare_select_fusion = f32[4,8,64,128]{3,2,1,0:T(8,128)} fusion(f32[4,8,64,128]{3,2,1,0:T(8,128)} %shard_map.56, s32[4,8,64]{2,1,0:T(8,128)S(1)} %copy-done.3, s32[128]{0:T(128)S(1)} %add_abs_fusion), kind=kLoop, calls=%fused_computation.1 | loop fusion | flops 524288 | bytes 2105856 | tf_op jit(solution)/shard_map/jit(_where)/select_n | solution.py:403
  (1 shorter events, 0.0 us)
Async XLA Ops:
  0.0 2.5 %copy-start.2 = (s32[4]{0:T(128)S(1)}, s32[4]{0:T(128)}, u32[]{:S(2)}) copy-start(s32[4]{0:T(128)} %blocks_ref.1) | copy-start | bytes 52
  2.5 4.7 %copy-start = (bf16[4,64,2,2048]{3,1,2,0:T(8,128)(2,1)}, bf16[4,64,2,2048]{3,1,2,0:T(8,128)(2,1)S(1)}, u32[]{:S(2)}) copy-start(bf16[4,64,2,2048]{3,1,2,0:T(8,128)(2,1)S(1)} %copy.8) | copy-start | bytes 6291460
  7.2 1.3 %copy-start.1 = (bf16[4,64,16,256]{3,2,1,0:T(8,128)(2,1)}, bf16[4,64,16,256]{3,2,1,0:T(8,128)(2,1)S(1)}, u32[]{:S(2)}) copy-start(bf16[4,64,16,256]{3,2,1,0:T(8,128)(2,1)S(1)} %shard_map.55) | copy-start | bytes 6291460
  8.5 86.0 %copy-start.3 = (s32[4,8,64]{2,1,0:T(8,128)S(1)}, s32[4,8,64]{2,1,0:T(8,128)}, u32[]{:S(2)}) copy-start(s32[4,8,64]{2,1,0:T(8,128)} %param.8) | copy-start | bytes 24580

commit v4 on v3

--- a/solution.py
+++ b/solution.py
@@ -175,7 +175,10 @@
     def _(s):
         to_core(s).wait_recv()
         half[s] = lax.select(owners_ref[s] == me, own_ref[s, pl.ds(2 * core, 2)], from_core[s])
-        to_cross(s).start()
+
+        @pl.when(s < 2)
+        def _():
+            to_cross(s).start()
 
     @pl.loop(0, bins // LANES)
     def _(q):
@@ -223,20 +226,23 @@
         lax.fori_loop(0, groups, group_step, 0, unroll=2)
 
     def lag_part(s):
-        for pair in range(sources // 2):
-            block = jnp.dot(
-                lag_ref[...],
-                cross_spectra[s, :, pair * 2 * LANES : (pair + 1) * 2 * LANES],
-                preferred_element_type=jnp.float32,
-            )
-            turned = block.T
-            lags = turned.shape[1] // 2
-            for k in range(2):
-                top = k * LANES
-                made[s, 2 * pair + k] = (
-                    turned[top : top + receivers, :lags]
-                    + turned[top + receivers : top + 2 * receivers, lags:]
+        for j in list(range(1, members)) + [0]:
+            for p in range(kept // 2):
+                pair = ((win + j) % members) * (kept // 2) + p
+                at = pl.ds(pl.multiple_of(pair * 2 * LANES, 2 * LANES), 2 * LANES)
+                block = jnp.dot(
+                    lag_ref[...], cross_spectra[s, :, at], preferred_element_type=jnp.float32
                 )
+                turned = block.T
+                lags = turned.shape[1] // 2
+                for k in range(2):
+                    top = k * LANES
+                    made[s, 2 * pair + k] = (
+                        turned[top : top + receivers, :lags]
+                        + turned[top + receivers : top + 2 * receivers, lags:]
+                    )
+            if j > 0:
+                add_up(s, j).start()
 
     def low_side(s):
         @pl.when(has_low)
@@ -260,6 +266,11 @@
 
     def enter(s):
         to_cross(s).wait_recv()
+
+        @pl.when(s + 2 < steps)
+        def _():
+            to_cross(s + 2).start()
+
         value = lax.select((owners_ref[s] // 2) % 2 == cross, half[s, cross], from_cross[s])
         quarter[s] = value
 
@@ -290,6 +301,13 @@
         @pl.when(jnp.logical_not(near_low))
         def _():
             low_side(s)
+
+    inner = (line > 0) & (line < length - 1)
+
+    def settle(s):
+        @pl.when(jnp.logical_not(inner))
+        def _():
+            far_side(s)
 
         got[s, mine] = lax.select(owners_ref[s] // 4 <= line, to_high[s], to_low[s])
         share(s).start()
@@ -299,38 +317,41 @@
         share(s).wait_recv()
         last(s, 1, theirs).start()
 
-    @pl.loop(0, steps + 2)
+    @pl.loop(0, steps + 4)
     def _(t):
+        @pl.when(t >= 4)
+        def _():
+            pass_on(t - 4)
+
+        @pl.when((t >= 3) & (t < steps + 3))
+        def _():
+            settle(t - 3)
+
+        @pl.when((t >= 2) & (t < steps + 2) & inner)
+        def _():
+            far_side(t - 2)
+
+        @pl.when((t >= 1) & (t < steps + 1))
+        def _():
+            near_side(t - 1)
+
         @pl.when(t < steps)
         def _():
             enter(t)
 
-        @pl.when((t >= 1) & (t <= steps))
-        def _():
-            near_side(t - 1)
-
-        @pl.when(t >= 2)
-        def _():
-            far_side(t - 2)
-
-            @pl.when(t >= 3)
-            def _():
-                pass_on(t - 3)
-
-            cross_part(t - 2, mine)
-
-    pass_on(steps - 1)
-
-    @pl.loop(0, steps)
-    def _(s):
-        cross_part(s, theirs)
-        for which in range(2):
-            last(s, which, mine).wait_recv()
-        cross_part(s, 2 * (1 - core))
-        cross_part(s, 2 * (1 - core) + 1)
-        lag_part(s)
-        for j in range(1, members):
-            add_up(s, j).start()
+        @pl.when((t >= 3) & (t < steps + 3))
+        def _():
+            cross_part(t - 3, mine)
+
+        @pl.when(t >= 4)
+        def _():
+            s = t - 4
+            cross_part(s, theirs)
+            for which in range(2):
+                last(s, which, mine).wait_recv()
+            cross_part(s, 2 * (1 - core))
+            cross_part(s, 2 * (1 - core) + 1)
+            lag_part(s)
 
     @pl.loop(0, steps)
     def _(s):

time: 97.2 us -> 93.2 us (0.959)
  Pallas kernels: 90.6 us -> 86.6 us
    pallas_call x1, Pallas kernels: 86 us -> 82 us  [main(): pl.pallas_call(functools.partial(main_kernel, length=lax.axis_size('chan'...]
where the time goes in v4:
time: 93.2 us; the launch traced here: 93.1 us
  Pallas kernels  86.6 us (93%)
  local copies, waits for them, and re-layouts  3.82 us (4%)
  other arithmetic  2.54 us (3%)
    pallas_call x1, Pallas kernels, main(): pl.pallas_call(functools.partial(main_kernel, length=lax.axis_size('chan'...  82 us
    pallas_call x1, Pallas kernels, prepare(): pl.pallas_call(functools.partial(prepare_kernel, run=run), out_shape=jax....  4.64 us
    unnamed x9, local copies, waits for them, and re-layouts  3.82 us
    select_n x1, other arithmetic, body(): return jnp.where(inside, stacked, jnp.float32(0.0))  2.53 us

profile of v4, /device:TPU:0, one launch (start us, length us, event | category | flops | bytes accessed | tf_op | source)
XLA Modules:
  0.0 93.1 jit_solution(3982006684912018873)
XLA Ops:
  0.0 0.0 copy-start.2
  0.0 2.5 %copy.8 = bf16[4,64,2,2048]{3,1,2,0:T(8,128)(2,1)S(1)} copy(bf16[4,64,2,2048]{3,2,1,0:T(2,128)(2,1)} %param.5) | data formatting | bytes 4194304 | tf_op args[0]
  2.5 0.0 copy-start
  2.5 0.0 copy-done.2
  2.5 4.6 %shard_map.55 = bf16[4,64,16,256]{3,2,1,0:T(8,128)(2,1)S(1)} custom-call(s32[4]{0:T(128)S(1)} %copy-done.2, bf16[4,2,64,2048]{3,2,1,0:T(8,128)(2,1)S(1)} %bitcast.4), custom_call_target="tpu_custom_call" | custom-call | tf_op jit(solution)/shard_map/pallas_call | solution.py:63
  7.2 0.0 copy-done
  7.2 0.0 copy-start.1
  7.2 1.3 %copy-done.1 = bf16[4,64,16,256]{3,2,1,0:T(8,128)(2,1)} copy-done((bf16[4,64,16,256]{3,2,1,0:T(8,128)(2,1)}, bf16[4,64,16,256]{3,2,1,0:T(8,128)(2,1)S(1)}, u32[]{:S(2)}) %copy-start.1) | copy-done | bytes 2097176
  8.5 0.0 copy-start.3
  8.5 82.0 %shard_map.56 = f32[4,8,64,128]{3,2,1,0:T(8,128)} custom-call(s32[4]{0:T(128)} %owners_ref.1, bf16[4,4,16,16,256]{4,3,2,1,0:T(8,128)(2,1)} %bitcast.6, bf16[4,2,64,2048]{3,2,1,0:T(8,128)(2,1)} %bitcast.5, bf16[256,2048]{1,0:T(8,128)(2,1)} %constant.7.clone.lag_ref), custom_call_target="tpu_custom_call" | custom-call | tf_op jit(solution)/shard_map/pallas_call | solution.py:387
  90.5 0.0 copy-done.3
  90.5 2.5 %compare_select_fusion = f32[4,8,64,128]{3,2,1,0:T(8,128)} fusion(f32[4,8,64,128]{3,2,1,0:T(8,128)} %shard_map.56, s32[4,8,64]{2,1,0:T(8,128)S(1)} %copy-done.3, s32[128]{0:T(128)S(1)} %add_abs_fusion), kind=kLoop, calls=%fused_computation.1 | loop fusion | flops 524288 | bytes 2105856 | tf_op jit(solution)/shard_map/jit(_where)/select_n | solution.py:424
  (1 shorter events, 0.0 us)
Async XLA Ops:
  0.0 2.5 %copy-start.2 = (s32[4]{0:T(128)S(1)}, s32[4]{0:T(128)}, u32[]{:S(2)}) copy-start(s32[4]{0:T(128)} %blocks_ref.1) | copy-start | bytes 52
  2.5 4.7 %copy-start = (bf16[4,64,2,2048]{3,1,2,0:T(8,128)(2,1)}, bf16[4,64,2,2048]{3,1,2,0:T(8,128)(2,1)S(1)}, u32[]{:S(2)}) copy-start(bf16[4,64,2,2048]{3,1,2,0:T(8,128)(2,1)S(1)} %copy.8) | copy-start | bytes 6291460
  7.2 1.3 %copy-start.1 = (bf16[4,64,16,256]{3,2,1,0:T(8,128)(2,1)}, bf16[4,64,16,256]{3,2,1,0:T(8,128)(2,1)S(1)}, u32[]{:S(2)}) copy-start(bf16[4,64,16,256]{3,2,1,0:T(8,128)(2,1)S(1)} %shard_map.55) | copy-start | bytes 6291460
  8.5 82.0 %copy-start.3 = (s32[4,8,64]{2,1,0:T(8,128)S(1)}, s32[4,8,64]{2,1,0:T(8,128)}, u32[]{:S(2)}) copy-start(s32[4,8,64]{2,1,0:T(8,128)} %param.8) | copy-start | bytes 24580

commit v5 on v4

--- a/solution.py
+++ b/solution.py
@@ -223,7 +223,7 @@
                 cross_spectra[s, pl.ds(base + run, run), at] = one[:, LANES:]
             return carry
 
-        lax.fori_loop(0, groups, group_step, 0, unroll=2)
+        lax.fori_loop(0, groups, group_step, 0, unroll=8)
 
     def lag_part(s):
         for j in list(range(1, members)) + [0]:

time: 93.2 us -> 78 us (0.84)
  Pallas kernels: 86.6 us -> 71.4 us
    pallas_call x1, Pallas kernels: 82 us -> 66.7 us  [main(): pl.pallas_call(functools.partial(main_kernel, length=lax.axis_size('chan'...]
where the time goes in v5:
time: 78 us; the launch traced here: 77.8 us
  Pallas kernels  71.4 us (92%)
  local copies, waits for them, and re-layouts  3.82 us (5%)
  other arithmetic  2.54 us (3%)
    pallas_call x1, Pallas kernels, main(): pl.pallas_call(functools.partial(main_kernel, length=lax.axis_size('chan'...  66.7 us
    pallas_call x1, Pallas kernels, prepare(): pl.pallas_call(functools.partial(prepare_kernel, run=run), out_shape=jax....  4.64 us
    unnamed x9, local copies, waits for them, and re-layouts  3.82 us
    select_n x1, other arithmetic, body(): return jnp.where(inside, stacked, jnp.float32(0.0))  2.53 us

profile of v5, /device:TPU:0, one launch (start us, length us, event | category | flops | bytes accessed | tf_op | source)
XLA Modules:
  0.0 77.8 jit_solution(1403833443237303608)
XLA Ops:
  0.0 0.0 copy-start.2
  0.0 2.5 %copy.8 = bf16[4,64,2,2048]{3,1,2,0:T(8,128)(2,1)S(1)} copy(bf16[4,64,2,2048]{3,2,1,0:T(2,128)(2,1)} %param.5) | data formatting | bytes 4194304 | tf_op args[0]
  2.5 0.0 copy-start
  2.5 0.0 copy-done.2
  2.5 4.6 %shard_map.55 = bf16[4,64,16,256]{3,2,1,0:T(8,128)(2,1)S(1)} custom-call(s32[4]{0:T(128)S(1)} %copy-done.2, bf16[4,2,64,2048]{3,2,1,0:T(8,128)(2,1)S(1)} %bitcast.4), custom_call_target="tpu_custom_call" | custom-call | tf_op jit(solution)/shard_map/pallas_call | solution.py:63
  7.2 0.0 copy-done
  7.2 0.0 copy-start.1
  7.2 1.3 %copy-done.1 = bf16[4,64,16,256]{3,2,1,0:T(8,128)(2,1)} copy-done((bf16[4,64,16,256]{3,2,1,0:T(8,128)(2,1)}, bf16[4,64,16,256]{3,2,1,0:T(8,128)(2,1)S(1)}, u32[]{:S(2)}) %copy-start.1) | copy-done | bytes 2097176
  8.5 0.0 copy-start.3
  8.5 66.7 %shard_map.56 = f32[4,8,64,128]{3,2,1,0:T(8,128)} custom-call(s32[4]{0:T(128)} %owners_ref.1, bf16[4,4,16,16,256]{4,3,2,1,0:T(8,128)(2,1)} %bitcast.6, bf16[4,2,64,2048]{3,2,1,0:T(8,128)(2,1)} %bitcast.5, bf16[256,2048]{1,0:T(8,128)(2,1)} %constant.7.clone.lag_ref), custom_call_target="tpu_custom_call" | custom-call | tf_op jit(solution)/shard_map/pallas_call | solution.py:387
  75.2 0.0 copy-done.3
  75.3 2.5 %compare_select_fusion = f32[4,8,64,128]{3,2,1,0:T(8,128)} fusion(f32[4,8,64,128]{3,2,1,0:T(8,128)} %shard_map.56, s32[4,8,64]{2,1,0:T(8,128)S(1)} %copy-done.3, s32[128]{0:T(128)S(1)} %add_abs_fusion), kind=kLoop, calls=%fused_computation.1 | loop fusion | flops 524288 | bytes 2105856 | tf_op jit(solution)/shard_map/jit(_where)/select_n | solution.py:424
  (1 shorter events, 0.0 us)
Async XLA Ops:
  0.0 2.5 %copy-start.2 = (s32[4]{0:T(128)S(1)}, s32[4]{0:T(128)}, u32[]{:S(2)}) copy-start(s32[4]{0:T(128)} %blocks_ref.1) | copy-start | bytes 52
  2.5 4.7 %copy-start = (bf16[4,64,2,2048]{3,1,2,0:T(8,128)(2,1)}, bf16[4,64,2,2048]{3,1,2,0:T(8,128)(2,1)S(1)}, u32[]{:S(2)}) copy-start(bf16[4,64,2,2048]{3,1,2,0:T(8,128)(2,1)S(1)} %copy.8) | copy-start | bytes 6291460
  7.2 1.3 %copy-start.1 = (bf16[4,64,16,256]{3,2,1,0:T(8,128)(2,1)}, bf16[4,64,16,256]{3,2,1,0:T(8,128)(2,1)S(1)}, u32[]{:S(2)}) copy-start(bf16[4,64,16,256]{3,2,1,0:T(8,128)(2,1)S(1)} %shard_map.55) | copy-start | bytes 6291460
  8.5 66.7 %copy-start.3 = (s32[4,8,64]{2,1,0:T(8,128)S(1)}, s32[4,8,64]{2,1,0:T(8,128)}, u32[]{:S(2)}) copy-start(s32[4,8,64]{2,1,0:T(8,128)} %param.8) | copy-start | bytes 24580
